TPU v7x, 128 devices: a whole 4x4x4 slice. The times are simulated.
128 devices in a mesh: lat: 8 (over z, core), lon: 16 (over x, y).
Axes of the slice: x: 4, y: 4, z: 4, core: 2. Of those that a mesh axis runs over, the one named last changes fastest.
Arguments:
- latents: bfloat16 [128, 256, 256], P('lat', 'lon'), may hold values from -6 to 6
- conv_weight: bfloat16 [9, 256, 256], replicated, may hold values from -0.125 to 0.125
- map_weight: bfloat16 [256, 1024], replicated, may hold values from -0.375 to 0.375
- map_bias: float32 [1024], replicated, may hold values from -6 to 6
- input_weight: float32 [3, 512], replicated, may hold values from -3.5 to 3.5
- hidden_weight: bfloat16 [1, 512, 512], replicated, may hold values from -0.25 to 0.25
- output_weight: float32 [512], replicated, may hold values from -0.25 to 0.25
- hit_owner: int32 [12288], P(('lat', 'lon')), may hold values from 0 to 127, as said below
- serve_block: int32 [128, 128], P(('lat', 'lon')), may hold values from -1 to 1, as said below
- query_grid: int32 [3, 786432], P(None, ('lat', 'lon')), may hold values from 0 to 127, as said below
- cotangent: float32 [786432], P(('lat', 'lon')), may hold values from -6 to 6
Outputs:
- latent_grad: float32 [128, 256, 256], P('lat', 'lon')
- conv_grad: float32 [9, 256, 256], replicated
- map_grad: float32 [256, 1024], replicated
- map_bias_grad: float32 [1024], replicated
- input_grad: float32 [3, 512], replicated
- hidden_grad: float32 [1, 512, 512], replicated
- output_grad: float32 [512], replicated
Inputs may be any that keep to these rules, and one draw needn't show every extreme that they name: `hit_owner`: each device's 96 entries name distinct devices, numbered lat index times the size of lon plus lon index. `serve_block`: entry [o, r] is a block of device o, 0 to 1, when the list of device r names o, and -1 otherwise. `query_grid`: row 0 is the cell within the block (row-major over 8 rows of 16 cells), row 1 the sub-cell (0 to 35, row-major), row 2 the level (0 to 36).
All inputs are finite; a program needn't handle non-finite values.
Results may differ from a plain program's by a relative error of at most 0.0095.
Values may be sent and summed in bfloat16 or wider, within the bound.
A program may use at most 128 MiB of HBM per device.

v0:
```python
import jax
import jax.numpy as jnp
from jax import lax
from jax.sharding import PartitionSpec as P

BLOCK = 128
LEVELS = 37
SUB = 6


OMEGA = 30.0


def padded_2(block, sides, width):
    for axis, dim in sides:
        count = lax.axis_size(axis)
        forward = [(i, i + 1) for i in range(count - 1)]
        forward.append((count - 1, 0))
        backward = [(target, source) for source, target in forward]
        low = lax.ppermute(
            lax.slice_in_dim(block, block.shape[dim] - width, None, axis=dim), axis, forward
        )
        high = lax.ppermute(lax.slice_in_dim(block, 0, width, axis=dim), axis, backward)
        block = jnp.concatenate([low, block, high], axis=dim)
    return block


def conv_apply(padded, kernel, row_count, col_count, flipped):
    channels = padded.shape[-1]
    result = jnp.zeros((row_count * col_count, kernel.shape[-1]), jnp.float32)
    for shift_a in (-1, 0, 1):
        for shift_b in (-1, 0, 1):
            tap_index = (shift_a + 1) * 3 + shift_b + 1
            if flipped:
                window = padded[
                    1 - shift_a : 1 - shift_a + row_count, 1 - shift_b : 1 - shift_b + col_count
                ]
                matrix = kernel[tap_index].T
            else:
                window = padded[
                    1 + shift_a : 1 + shift_a + row_count, 1 + shift_b : 1 + shift_b + col_count
                ]
                matrix = kernel[tap_index]
            result = result + jnp.dot(
                window.reshape(row_count * col_count, channels),
                matrix,
                preferred_element_type=jnp.float32,
            )
    return result


def conv_weight_grad(padded, grads, row_count, col_count):
    flat_grads = grads.reshape(row_count * col_count, -1)
    pieces = []
    for shift_a in (-1, 0, 1):
        for shift_b in (-1, 0, 1):
            window = padded[
                1 + shift_a : 1 + shift_a + row_count, 1 + shift_b : 1 + shift_b + col_count
            ]
            window = window.reshape(row_count * col_count, -1)
            pieces.append(jnp.dot(window.T, flat_grads, preferred_element_type=jnp.float32))
    return jnp.stack(pieces)


def close_poles(padded, lat_pos, lat_parts):
    top_rim = jnp.where(lat_pos == 0, jnp.zeros_like(padded[:1]), padded[:1])
    bottom_rim = jnp.where(lat_pos == lat_parts - 1, jnp.zeros_like(padded[-1:]), padded[-1:])
    return jnp.concatenate([top_rim, padded[1:-1], bottom_rim], axis=0)


def split_parts(values):
    upper = values.astype(jnp.bfloat16)
    lower = (values - upper.astype(jnp.float32)).astype(jnp.bfloat16)
    return (upper, lower)


def query_coords(
    cell_index, sub_index, level_index, lat_base, lon_base, lon_tile, lat_cells, lon_cells
):
    row_index = lat_base[:, None] + cell_index // lon_tile
    col_index = lon_base[:, None] + cell_index % lon_tile
    lat_coord = ((row_index * SUB + sub_index // SUB).astype(jnp.float32) + 0.5) / (
        lat_cells * SUB
    ) * 2.0 - 1.0
    lon_coord = ((col_index * SUB + sub_index % SUB).astype(jnp.float32) + 0.5) / (
        lon_cells * SUB
    ) * 2.0 - 1.0
    level_coord = (level_index.astype(jnp.float32) + 0.5) / LEVELS * 2.0 - 1.0
    return jnp.stack([lat_coord.reshape(-1), lon_coord.reshape(-1), level_coord.reshape(-1)])


def sine_grads(
    features, coords, cotan_rows, map_weight, map_bias, input_weight, hidden_weight, output_weight
):
    hidden_size = input_weight.shape[1]
    depth_count = map_weight.shape[1] // hidden_size
    shifts = jnp.dot(features, map_weight, preferred_element_type=jnp.float32) + map_bias
    linear = (
        coords[0][:, None] * input_weight[0]
        + coords[1][:, None] * input_weight[1]
        + coords[2][:, None] * input_weight[2]
    )
    preacts = [OMEGA * linear + shifts[:, :hidden_size]]
    layer_index = 1
    previous = jnp.sin(preacts[-1]).astype(jnp.bfloat16)
    inputs_rounded = [previous]
    preacts.append(
        jnp.dot(previous, hidden_weight[layer_index - 1], preferred_element_type=jnp.float32)
        + shifts[:, layer_index * hidden_size : (layer_index + 1) * hidden_size]
    )
    last_act = jnp.sin(preacts[-1])
    output_grad = jnp.dot(cotan_rows, last_act, precision=lax.Precision.HIGHEST)
    act_grad = cotan_rows[:, None] * output_weight[None, :]
    pre_grads = [None] * depth_count
    rounded_grads = [None] * depth_count
    hidden_grads = [None] * (depth_count - 1)
    for layer_index in range(depth_count - 1, -1, -1):
        pre_grads[layer_index] = act_grad * jnp.cos(preacts[layer_index])
        rounded_grads[layer_index] = pre_grads[layer_index].astype(jnp.bfloat16)
        if layer_index > 0:
            hidden_grads[layer_index - 1] = jnp.dot(
                inputs_rounded[layer_index - 1].T,
                rounded_grads[layer_index],
                preferred_element_type=jnp.float32,
            )
            act_grad = jnp.dot(
                rounded_grads[layer_index],
                hidden_weight[layer_index - 1].T,
                preferred_element_type=jnp.float32,
            )
    input_grad = OMEGA * jnp.dot(coords, pre_grads[0], precision=lax.Precision.HIGHEST)
    mod_grads = jnp.concatenate(rounded_grads, axis=1)
    bias_grad = jnp.sum(jnp.concatenate(pre_grads, axis=1), axis=0)
    map_grad = jnp.dot(features.T, mod_grads, preferred_element_type=jnp.float32)
    feature_grads = jnp.dot(mod_grads, map_weight.T, preferred_element_type=jnp.float32)
    return (feature_grads, (map_grad, bias_grad, input_grad, jnp.stack(hidden_grads), output_grad))


def run_groups(
    blocks,
    cell_index,
    sub_index,
    level_index,
    lat_base,
    lon_base,
    cotan_rows,
    weights,
    lon_tile,
    lat_cells,
    lon_cells,
):
    group_count = blocks.shape[0]
    block_rows = blocks.shape[1]
    channels = blocks.shape[2]
    step_size = 8
    turns = group_count // step_size

    def split_turns(source):
        return source.reshape((turns, step_size) + source.shape[1:])

    inputs = (
        split_turns(blocks),
        split_turns(cell_index),
        split_turns(sub_index),
        split_turns(level_index),
        split_turns(lat_base),
        split_turns(lon_base),
        split_turns(cotan_rows),
    )
    map_weight, map_bias, input_weight, hidden_weight, output_weight = weights
    initial = (
        jnp.zeros(map_weight.shape, jnp.float32),
        jnp.zeros(map_bias.shape, jnp.float32),
        jnp.zeros(input_weight.shape, jnp.float32),
        jnp.zeros(hidden_weight.shape, jnp.float32),
        jnp.zeros(output_weight.shape, jnp.float32),
    )

    def advance(grad_totals, slices):
        block_part, cell_part, sub_part, level_part, latb_part, lonb_part, cotan_part = slices
        onehot = (
            cell_part[:, :, None] == jnp.arange(block_rows, dtype=jnp.int32)[None, None, :]
        ).astype(jnp.bfloat16)
        features_q = jnp.einsum(
            "hgb,hbc->hgc", onehot, block_part, preferred_element_type=jnp.float32
        ).astype(jnp.bfloat16)
        coords = query_coords(
            cell_part, sub_part, level_part, latb_part, lonb_part, lon_tile, lat_cells, lon_cells
        )
        feature_grads, grads = sine_grads(
            features_q.reshape(-1, channels),
            coords,
            cotan_part.reshape(-1),
            map_weight,
            map_bias,
            input_weight,
            hidden_weight,
            output_weight,
        )
        upper, lower = split_parts(
            feature_grads.reshape(onehot.shape[0], onehot.shape[1], channels)
        )
        block_grads = jnp.einsum(
            "hgb,hgc->hbc", onehot, upper, preferred_element_type=jnp.float32
        ) + jnp.einsum("hgb,hgc->hbc", onehot, lower, preferred_element_type=jnp.float32)
        return (jax.tree.map(jnp.add, grad_totals, grads), block_grads)

    grad_totals, block_grads = lax.scan(advance, initial, inputs)
    return (block_grads.reshape(group_count, block_rows, channels), grad_totals)


def on_device(
    latents,
    conv_weight,
    map_weight,
    map_bias,
    input_weight,
    hidden_weight,
    output_weight,
    hit_owner,
    serve_block,
    query_grid,
    cotangent,
):
    lat_tile, lon_tile, channels = latents.shape
    lat_parts = lax.axis_size("lat")
    lon_parts = lax.axis_size("lon")
    dev_count = lat_parts * lon_parts
    lat_cells = lat_tile * lat_parts
    lon_cells = lon_tile * lon_parts
    block_rows = BLOCK
    tile_blocks = lat_tile * lon_tile // block_rows
    rows_per_block = block_rows // lon_tile
    lat_pos = lax.axis_index("lat")
    padded = close_poles(padded_2(latents, (("lat", 0), ("lon", 1)), 1), lat_pos, lat_parts)
    features = conv_apply(padded, conv_weight, lat_tile, lon_tile, False).astype(jnp.bfloat16)
    own_blocks = features.reshape(tile_blocks, block_rows * channels)
    serve_row = serve_block[0]
    selector = (serve_row[:, None] == jnp.arange(tile_blocks, dtype=jnp.int32)[None, :]).astype(
        jnp.bfloat16
    )
    slot_blocks = jnp.dot(selector, own_blocks, preferred_element_type=jnp.float32).astype(
        jnp.bfloat16
    )
    slot_blocks = slot_blocks.reshape(dev_count, block_rows, channels)
    weights = (map_weight, map_bias, input_weight, hidden_weight, output_weight)
    hit_count = hit_owner.shape[0]
    group_size = cotangent.shape[0] // hit_count
    got_blocks, got_index = (
        lax.all_to_all(slot_blocks, ("lat", "lon"), split_axis=0, concat_axis=0, tiled=True),
        lax.all_to_all(
            serve_block.reshape(dev_count, 1),
            ("lat", "lon"),
            split_axis=0,
            concat_axis=0,
            tiled=True,
        ),
    )
    hit_blocks = got_blocks[hit_owner]
    hit_index = got_index[hit_owner, 0]
    lat_base = hit_owner // lon_parts * lat_tile + hit_index * rows_per_block
    lon_base = hit_owner % lon_parts * lon_tile
    grid_groups = query_grid.reshape(3, hit_count, group_size)
    hit_grads, grad_totals = run_groups(
        hit_blocks,
        grid_groups[0],
        grid_groups[1],
        grid_groups[2],
        lat_base,
        lon_base,
        cotangent.reshape(hit_count, group_size),
        weights,
        lon_tile,
        lat_cells,
        lon_cells,
    )
    outgoing = (
        jnp.zeros((dev_count, block_rows, channels), jnp.float32).at[hit_owner].set(hit_grads)
    )
    slot_grads = lax.all_to_all(outgoing, ("lat", "lon"), split_axis=0, concat_axis=0, tiled=True)
    slot_upper, slot_lower = split_parts(slot_grads.reshape(dev_count, block_rows * channels))
    tile_grads = jnp.dot(selector.T, slot_upper, preferred_element_type=jnp.float32) + jnp.dot(
        selector.T, slot_lower, preferred_element_type=jnp.float32
    )
    feature_grad = tile_grads.reshape(lat_tile, lon_tile, channels).astype(jnp.bfloat16)
    padded_grad = close_poles(
        padded_2(feature_grad, (("lat", 0), ("lon", 1)), 1), lat_pos, lat_parts
    )
    latent_grad = conv_apply(padded_grad, conv_weight, lat_tile, lon_tile, True).reshape(
        lat_tile, lon_tile, channels
    )
    conv_local = conv_weight_grad(padded, feature_grad, lat_tile, lon_tile)
    totals = lax.psum(
        (
            conv_local,
            grad_totals[0],
            grad_totals[1],
            grad_totals[2],
            grad_totals[3],
            grad_totals[4],
        ),
        ("lat", "lon"),
    )
    grad_scale = float(hit_count * group_size * dev_count) ** (-0.5)
    return (
        latent_grad,
        totals[0] * grad_scale,
        totals[1] * grad_scale,
        totals[2] * grad_scale,
        totals[3] * grad_scale,
        totals[4] * grad_scale,
        totals[5] * grad_scale,
    )


def solution(mesh):
    placed = (
        P("lat", "lon", None),
        P(),
        P(),
        P(),
        P(),
        P(),
        P(),
        P(("lat", "lon")),
        P(("lat", "lon"), None),
        P(None, ("lat", "lon")),
        P(("lat", "lon")),
    )
    return jax.shard_map(
        on_device,
        mesh=mesh,
        in_specs=placed,
        out_specs=(P("lat", "lon", None), P(), P(), P(), P(), P(), P()),
        check_vma=False,
    )
```

profile of v0, /device:TPU:1, one launch (start us, length us, event | category | flops | bytes accessed | tf_op | source)
XLA Modules:
  0.0 1199.0 jit_solution(17336542981710766287)
XLA Ops:
  12.4 10.2 all-to-all-start.1
  37.7 9.2 copy.36
  46.9 10.9 all-to-all-start
  65.8 92.8 %all-to-all-done = bf16[128,128,256]{2,1,0:T(8,128)(2,1)} async-done(((bf16[128,128,256]{2,1,0:T(8,128)(2,1)}), bf16[128,128,256]{2,1,0:T(8,128)(2,1)}, u32[]{:S(2)}, u32[]{:S(2)}) %all-to-all-start) | async-done | bytes 8388640 | tf_op jit(solution)/shard_map/all_to_all | solution.py:250
  158.6 9.4 gather_fusion
  168.0 492.6 %while.24 = (s32[]{:T(128)}, f32[256,1024]{1,0:T(8,128)S(1)}, f32[1024]{0:T(1024)}, f32[3,512]{1,0:T(4,128)}, f32[1,512,512]{2,1,0:T(8,128)}, /*index=5*/f32[512...) while((s32[]{:T(128)}, f32[256,1024]{1,0:T(8,128)S(1)}, ...), condition=%wide.region_2.3_spmd.clone, body=%wide.region_0.2_spmd.clone.sunk | while | flops 1739577856 | bytes 41028000 | solution.py:208
  185.4 7.2 fusion.207
  225.7 7.2 fusion.207
  265.9 7.2 fusion.207
  306.2 7.2 fusion.207
  346.5 7.2 fusion.207
  386.8 7.2 fusion.207
  427.0 7.2 fusion.207
  467.3 7.2 fusion.207
  507.6 7.2 fusion.207
  547.9 7.2 fusion.207
  588.1 7.2 fusion.207
  628.4 7.2 fusion.207
  660.7 7.9 broadcast_in_dim.42
  668.6 24.5 %scatter_fusion = f32[128,128,256]{2,1,0:T(8,128)} fusion(f32[128,128,256]{2,1,0:T(8,128)} %broadcast_in_dim.42, s32[96]{0:T(128)S(1)} %copy-done.34, f32[96,128,256]{2,1,0:T(8,128)} %bitcast.249), kind=kCustom, calls=%fused_computation.2 | custom fusion | bytes 37749120 | tf_op jit(solution)/shard_map/scatter | solution.py:278
  693.1 9.7 all-to-all-start.2
  702.8 296.6 %all-reduce.1 = (f32[1024]{0:T(1024)S(1)}, f32[3,512]{1,0:T(4,128)S(1)}, f32[512]{0:T(512)S(1)}) all-reduce(f32[1024]{0:T(1024)S(1)} %copy-done.20, f32[3,512]{1,0:T(4,128)S(1)} %copy-done.14, f32[512]{0:T(512)S(1)} %copy-done.23), channel_id=1, replica_groups=mesh['lat'=8,'lon'=16] {'lat','lon'}, use_global_device_ids=true, to_apply=%region_6.7 | all-reduce | flops 3072 | bytes 24576 | tf_op jit(solution)/shard_map/psum | solution.py:293
  1001.2 15.5 %copy.37 = f32[16,8,128,256]{3,1,2,0:T(8,128)S(1)} copy(f32[16,8,128,256]{3,2,1,0:T(8,128)} %bitcast.68) | data formatting | bytes 33554432
  1038.0 148.3 %all-reduce.5.cloned.1.call-done = (f32[9,256,256]{2,1,0:T(8,128)}, f32[256,1024]{1,0:T(8,128)}, f32[1,512,512]{2,1,0:T(8,128)}) async-done(((f32[9,256,256]{2,1,0:T(8,128)}, f32[256,1024]{1,0:T(8,128)}, f32[1,512,512]{2,1,0:T(8,128)}), (f32[9,256,256]{2,1,0:T(8,128)}, f32[256,1024]{1,0:T(8,128)}, f32[1,512,512]{2,1,0:T(8,128)})) %all-reduce.5.cloned.1.call-update) | async-done | bytes 4456464 | tf_op jit(solution)/shard_map/psum | solution.py:293
  (1026 shorter events, 450.1 us)
Async XLA Ops:
  7.2 23.1 %copy-start.2 = (bf16[9,256,256]{2,1,0:T(8,128)(2,1)S(1)}, bf16[9,256,256]{2,1,0:T(8,128)(2,1)}, u32[]{:S(2)}) copy-start(bf16[9,256,256]{2,1,0:T(8,128)(2,1)} %param.14) | copy-start | bytes 3538948
  8.0 14.6 %collective-permute-start = (bf16[1,16,256]{2,1,0:T(8,128)(2,1)S(1)}, bf16[1,16,256]{2,1,0:T(8,128)(2,1)S(1)}, u32[]{:S(2)}, u32[]{:S(2)}) collective-permute-start(bf16[1,16,256]{2,1,0:T(8,128)(2,1)S(1)} %get-tuple-element.488), channel_id=1, source_target_pairs={{0,16},{16,32},{32,48},{48,64},{64,80},{80,96},{96,112},{112,0},{1... | collective-permute-start | bytes 24584 | tf_op jit(solution)/shard_map/ppermute | solution.py:20
  11.0 12.6 %collective-permute-start.1 = (bf16[1,16,256]{2,1,0:T(8,128)(2,1)S(1)}, bf16[1,16,256]{2,1,0:T(8,128)(2,1)S(1)}, u32[]{:S(2)}, u32[]{:S(2)}) collective-permute-start(bf16[1,16,256]{2,1,0:T(8,128)(2,1)S(1)} %get-tuple-element.487), channel_id=1, source_target_pairs={{16,0},{32,16},{48,32},{64,48},{80,64},{96,80},{112,96},{0,112},{1... | collective-permute-start | bytes 24584 | tf_op jit(solution)/shard_map/ppermute | solution.py:23
  12.4 34.5 %all-to-all-start.1 = ((s32[128,1,1]{2,1,0:T(1,128)}), s32[128,1,1]{2,1,0:T(1,128)S(1)}, u32[]{:S(2)}, u32[]{:S(2)}) async-start(s32[128,1,1]{2,1,0:T(1,128)} %copy.30), calls=%async_computation.1 | async-start | bytes 131072 | tf_op jit(solution)/shard_map/all_to_all | solution.py:251
  23.6 6.3 collective-permute-start.2
  25.1 4.9 collective-permute-start.3
  46.9 11.6 copy-start.30
  46.9 12.3 %copy-start.24 = (s32[3,6144]{1,0:T(4,128)S(1)}, s32[3,6144]{1,0:T(4,128)}, u32[]{:S(2)}) copy-start(s32[3,6144]{1,0:T(4,128)} %param.22) | copy-start | bytes 221188
  46.9 111.7 %all-to-all-start = ((bf16[128,128,256]{2,1,0:T(8,128)(2,1)}), bf16[128,128,256]{2,1,0:T(8,128)(2,1)}, u32[]{:S(2)}, u32[]{:S(2)}) async-start(bf16[128,128,256]{2,1,0:T(8,128)(2,1)} %bitcast.246), calls=%async_computation | async-start | bytes 16777216 | tf_op jit(solution)/shard_map/all_to_all | solution.py:250
  65.8 102.2 %copy-start.1 = (bf16[256,1024]{1,0:T(8,128)(2,1)S(1)}, bf16[256,1024]{1,0:T(8,128)(2,1)}, u32[]{:S(2)}) copy-start(bf16[256,1024]{1,0:T(8,128)(2,1)} %param.15) | copy-start | bytes 1572868
  185.4 11.2 copy-start.4
  225.7 11.2 copy-start.4
  306.2 11.2 copy-start.4
  346.5 11.2 copy-start.4
  386.7 11.2 copy-start.4
  427.0 11.2 copy-start.4
  467.3 11.2 copy-start.4
  693.1 308.2 %all-to-all-start.2 = ((f32[128,128,256]{2,1,0:T(8,128)}), f32[128,128,256]{2,1,0:T(8,128)}, u32[]{:S(2)}, u32[]{:S(2)}) async-start(f32[128,128,256]{2,1,0:T(8,128)} %scatter_fusion), calls=%async_computation.2 | async-start | bytes 33554432 | tf_op jit(solution)/shard_map/all_to_all | solution.py:280
  702.8 483.6 %all-reduce.5.cloned.1.call-start = ((), (), s32[]{:S(2)}) async-start(), calls=%async_computation.3 | async-start | bytes 8912896 | tf_op jit(solution)/shard_map/psum | solution.py:293
  1001.2 15.5 %copy-start.32 = (s32[1,128]{1,0:T(1,128)S(1)}, s32[1,128]{1,0:T(1,128)}, u32[]{:S(2)}) copy-start(s32[1,128]{1,0:T(1,128)} %param.21) | copy-start | bytes 1540
  1020.5 8.5 collective-permute-start.5
  1021.6 7.4 collective-permute-start.4
  1029.1 6.0 collective-permute-start.6
  1029.2 5.9 collective-permute-start.7
  (224 other events, 1010.2 us)
Sparse Core Ops, SparseCore 0:
  1035.1 151.2 all-reduce.4
where the time goes:
time: 1210 us; the launch traced here: 1200 us
  matrix products  324 us (27%)
  blocking collectives  297 us (25%)
  waiting for transfers between devices  242 us (20%)
  local copies, waits for them, and re-layouts  201 us (17%)
  other arithmetic  63 us (5%)
  starting transfers between devices  45.4 us (4%)
  between operations  14.8 us (1%)
  loops' own time  13 us (1%)
    psum x1, blocking collectives, on_device(): lax.psum((conv_local, grad_totals[0], grad_totals[1], grad_totals[2], gra...  297 us
    psum x1, waiting for transfers between devices, on_device(): lax.psum((conv_local, grad_totals[0], grad_totals[1], grad_totals[2], gra...  148 us
    all_to_all x1, waiting for transfers between devices, on_device(): lax.all_to_all(slot_blocks, ('lat', 'lon'), split_axis=0, concat_axis=0,...  92.8 us
    dot_general x12, matrix products, sine_grads(): jnp.dot(previous, hidden_weight[layer_index - 1], preferred_element_type=...  86.1 us
    dot_general x12, matrix products, sine_grads(): jnp.dot(inputs_rounded[layer_index - 1].T, rounded_grads[layer_index], pr...  48.7 us
    dot_general x12, matrix products, sine_grads(): output_grad = jnp.dot(cotan_rows, last_act, precision=lax.Precision.HIGHEST)  47.5 us
    dot_general x12, matrix products, sine_grads(): jnp.dot(rounded_grads[layer_index], hidden_weight[layer_index - 1].T, pre...  45.9 us
    unnamed x46, local copies, waits for them, and re-layouts  25.7 us
  transfers between devices with their start and end apart: 12, of which 4 were waited for; matrix products, arithmetic and copies ran while one was open for 3% of the time, Pallas kernels for 0%

commit v1 on v0

v1 whole, which is shorter than its diff:
```python
import functools
import math

import jax
import jax.numpy as jnp
import numpy as np
from jax import lax
from jax.experimental import pallas as pl
from jax.experimental.pallas import tpu as pltpu
from jax.sharding import PartitionSpec as P

BLOCK = 128
LEVELS = 37
SUB = 6
OMEGA = 30.0
INV_TURN = float(1.0 / (2.0 * math.pi))
TURN = float(2.0 * math.pi)
TILE = 512
ROWS = 32


def _fit():
    nodes = np.cos((2 * np.arange(400) + 1) * np.pi / 800)
    r = (nodes + 1) / 4
    z = r * r
    sine = np.sqrt(2.0) * np.sin(np.pi * r)
    cosine = np.sqrt(2.0) * np.cos(np.pi * r)
    sa = np.stack([r * z**k for k in range(4)], 1)
    ca = np.stack([z**k for k in range(5)], 1)
    return (
        [float(v) for v in np.linalg.lstsq(sa, sine, rcond=None)[0]],
        [float(v) for v in np.linalg.lstsq(ca, cosine, rcond=None)[0]],
    )


SIN_C, COS_C = _fit()


def sincos_turns(t):
    r = t - jnp.round(t)
    z = r * r
    s = r * (SIN_C[0] + z * (SIN_C[1] + z * (SIN_C[2] + z * SIN_C[3])))
    c = COS_C[0] + z * (COS_C[1] + z * (COS_C[2] + z * (COS_C[3] + z * COS_C[4])))
    return s * c, 1.0 - s * s


def dot(a, b):
    return jnp.dot(a, b, preferred_element_type=jnp.float32)


def dot_nt(a, b):
    return lax.dot_general(a, b, (((1,), (1,)), ((), ())), preferred_element_type=jnp.float32)


def dot_tn(a, b):
    return lax.dot_general(a, b, (((0,), (0,)), ((), ())), preferred_element_type=jnp.float32)


def split2(v):
    hi = v.astype(jnp.bfloat16)
    return hi, (v - hi.astype(jnp.float32)).astype(jnp.bfloat16)


def split3(v):
    hi = v.astype(jnp.bfloat16).astype(jnp.float32)
    mid = (v - hi).astype(jnp.bfloat16).astype(jnp.float32)
    return hi, mid, v - hi - mid


def shifted(center, top, bottom, left, right):
    rows, cols, ch = center.shape
    total = (rows + 2) * cols
    mid = jnp.concatenate([top, center.reshape(rows * cols, ch), bottom], axis=0)
    mid32 = mid.astype(jnp.float32)
    col = lax.broadcasted_iota(jnp.int32, (rows + 2, cols, ch), 1)
    low = pltpu.roll(mid32, 1, 0).reshape(rows + 2, cols, ch)
    high = pltpu.roll(mid32, total - 1, 0).reshape(rows + 2, cols, ch)
    low = jnp.where(col == 0, left.astype(jnp.float32)[:, None, :], low)
    high = jnp.where(col == cols - 1, right.astype(jnp.float32)[:, None, :], high)
    return (
        low.reshape(total, ch).astype(jnp.bfloat16),
        mid,
        high.reshape(total, ch).astype(jnp.bfloat16),
    )


def main_kernel(
    dims,
    base_ref,
    q_ref,
    center_ref,
    top_ref,
    bottom_ref,
    left_ref,
    right_ref,
    convw_ref,
    mapw_ref,
    mapb_ref,
    inw_ref,
    hid_ref,
    outw_ref,
    fg_ref,
    conv_ref,
    map_ref,
    hidg_ref,
    small_ref,
    x3_ref,
    feat_ref,
    tab0_ref,
    tab1_ref,
    wcol_ref,
    rhs_ref,
    t_ref,
    c0_ref,
    d_ref,
    g_ref,
    og_ref,
):
    lat_cells, lon_cells = dims
    rows, cols, ch = center_ref.shape
    cells = rows * cols
    width = inw_ref.shape[1]
    tile = rhs_ref.shape[1]
    tiles = q_ref.shape[1] // tile
    f32 = jnp.float32
    bf16 = jnp.bfloat16

    x3 = shifted(center_ref[...], top_ref[...], bottom_ref[...], left_ref[...], right_ref[...])
    for b in range(3):
        x3_ref[:, b * ch : (b + 1) * ch] = x3[b]
    acc = dot(x3_ref[0:cells, :], convw_ref[0])
    for a in (1, 2):
        acc += dot(x3_ref[a * cols : a * cols + cells, :], convw_ref[a])
    feat_ref[...] = acc.astype(bf16)

    shift = dot(feat_ref[...], mapw_ref[...]) + mapb_ref[...]
    cell = lax.broadcasted_iota(jnp.int32, (cells, width), 0)
    row_f = (cell // cols).astype(f32)
    col_f = (cell % cols).astype(f32)
    lat_c = ((base_ref[0] + row_f) * SUB + 0.5) * (2.0 / (lat_cells * SUB)) - 1.0
    lon_c = ((base_ref[1] + col_f) * SUB + 0.5) * (2.0 / (lon_cells * SUB)) - 1.0
    lev_c = 1.0 / LEVELS - 1.0
    linear = (
        lat_c * inw_ref[0:1, :] + lon_c * inw_ref[1:2, :] + lev_c * inw_ref[2:3, :]
    )
    turn0 = (OMEGA * linear + shift[:, :width]) * INV_TURN
    turn0 = turn0 - jnp.round(turn0)
    hi, lo = split2(turn0.T)
    tab0_ref[:, 0:cells] = hi
    tab0_ref[:, cells : 2 * cells] = lo
    turn1 = shift[:, width:] * INV_TURN
    turn1 = (turn1 - jnp.round(turn1)) * TURN
    hi, lo = split2(turn1.T)
    tab1_ref[:, width : width + cells] = hi
    tab1_ref[:, width + cells : width + 2 * cells] = lo
    tab1_ref[:, 0:width] = hid_ref[...].astype(f32).T.astype(bf16)
    steps = (
        2.0 * OMEGA * INV_TURN / (lat_cells * SUB),
        2.0 * OMEGA * INV_TURN / (lon_cells * SUB),
        2.0 * OMEGA * INV_TURN / LEVELS,
    )
    parts = [split3(inw_ref[c : c + 1, :] * steps[c]) for c in range(3)]
    ext_row = lax.broadcasted_iota(jnp.int32, (128, width), 0)
    ext = jnp.zeros((128, width), f32)
    for level in range(3):
        for c in range(3):
            ext = jnp.where(ext_row == level * 3 + c, parts[c][level], ext)
    tab0_ref[:, 2 * cells : 2 * cells + 128] = ext.T.astype(bf16)
    wcol_ref[...] = jnp.broadcast_to(outw_ref[...], (128, width)).T

    oh0 = width
    oh1 = width + cells
    ex0 = width + 2 * cells
    rhs_ref[ex0:, :] = jnp.zeros((128, tile), bf16)
    g_ref[...] = jnp.zeros_like(g_ref)
    hidg_ref[...] = jnp.zeros_like(hidg_ref)
    og_ref[...] = jnp.zeros_like(og_ref)

    def step(i, carry):
        at = pl.ds(pl.multiple_of(i * tile, tile), tile)
        cell_q = q_ref[0:1, at]
        sub_r = q_ref[1:2, at]
        sub_c = q_ref[2:3, at]
        level = q_ref[3:4, at]
        cot = q_ref[4:5, at]
        for m in range(0, cells, 64):
            iota = (lax.broadcasted_iota(jnp.int32, (64, tile), 0) + m).astype(f32)
            onehot = jnp.where(iota == cell_q, 1.0, 0.0).astype(bf16)
            rhs_ref[oh0 + m : oh0 + m + 64, :] = onehot
            rhs_ref[oh1 + m : oh1 + m + 64, :] = onehot
        r = lax.broadcasted_iota(jnp.int32, (16, tile), 0)
        ints = jnp.where(r % 3 == 0, sub_r, jnp.where(r % 3 == 1, sub_c, level))
        rhs_ref[ex0 : ex0 + 16, :] = jnp.where(r < 9, ints, 0.0).astype(bf16)
        t_ref[...] = dot(tab0_ref[...], rhs_ref[oh0:, :])
        for m in range(0, width, ROWS):
            s, c = sincos_turns(t_ref[m : m + ROWS, :])
            rhs_ref[m : m + ROWS, :] = s.astype(bf16)
            c0_ref[m : m + ROWS, :] = c
        t_ref[...] = dot(tab1_ref[...], rhs_ref[0:ex0, :])
        for m in range(0, width, ROWS):
            s, c = sincos_turns(t_ref[m : m + ROWS, :] * INV_TURN)
            sw = s * cot
            w = wcol_ref[m : m + ROWS, :]
            og = og_ref[m : m + ROWS, :]
            cc = c * cot
            for n in range(0, tile, 128):
                og = og + sw[:, n : n + 128]
                d_ref[width + m : width + m + ROWS, n : n + 128] = (
                    cc[:, n : n + 128] * w
                ).astype(bf16)
            og_ref[m : m + ROWS, :] = og
        t_ref[...] = dot(hid_ref[...], d_ref[width:, :])
        for m in range(0, width, ROWS):
            d_ref[m : m + ROWS, :] = (
                t_ref[m : m + ROWS, :] * c0_ref[m : m + ROWS, :]
            ).astype(bf16)
        hidg_ref[...] += dot_nt(rhs_ref[0:width, :], d_ref[width:, :])
        g_ref[...] += dot_nt(rhs_ref[oh1 : ex0 + 16, :], d_ref[...])
        return carry

    lax.fori_loop(0, tiles, step, 0)

    g = g_ref[0:cells, :]
    hi, lo = split2(g)
    fg = (dot_nt(hi, mapw_ref[...]) + dot_nt(lo, mapw_ref[...])).astype(bf16)
    fg_ref[...] = fg
    feat_t = feat_ref[...].astype(f32).T.astype(bf16)
    map_ref[...] = dot(feat_t, hi) + dot(feat_t, lo)
    for a in range(3):
        conv_ref[a] = dot_tn(x3_ref[a * cols : a * cols + cells, :], fg)
    bias = jnp.sum(g, axis=0, keepdims=True)
    g0 = g[:, :width]
    ig0 = jnp.sum(lat_c * g0, axis=0, keepdims=True) + (2.0 / (lat_cells * SUB)) * g_ref[
        cells : cells + 1, :width
    ]
    ig1 = jnp.sum(lon_c * g0, axis=0, keepdims=True) + (2.0 / (lon_cells * SUB)) * g_ref[
        cells + 1 : cells + 2, :width
    ]
    ig2 = lev_c * bias[:, :width] + (2.0 / LEVELS) * g_ref[cells + 2 : cells + 3, :width]
    og = jnp.sum(og_ref[...].T, axis=0, keepdims=True)
    small_ref[0:1, :] = bias
    small_ref[1:2, 0:width] = OMEGA * ig0
    small_ref[1:2, width:] = OMEGA * ig1
    small_ref[2:3, 0:width] = OMEGA * ig2
    small_ref[2:3, width:] = og


def run_main(base, queries, center, halo, weights, dims):
    conv_weight, map_weight, map_bias, input_weight, hidden_weight, output_weight = weights
    rows, cols, ch = center.shape
    cells = rows * cols
    width = input_weight.shape[1]
    f32 = jnp.float32
    bf16 = jnp.bfloat16
    vmem = pl.BlockSpec(memory_space=pltpu.VMEM)
    return pl.pallas_call(
        functools.partial(main_kernel, dims),
        out_shape=(
            jax.ShapeDtypeStruct((cells, ch), bf16),
            jax.ShapeDtypeStruct((3, 3 * ch, ch), f32),
            jax.ShapeDtypeStruct((ch, 2 * width), f32),
            jax.ShapeDtypeStruct((width, width), f32),
            jax.ShapeDtypeStruct((3, 2 * width), f32),
        ),
        in_specs=[pl.BlockSpec(memory_space=pltpu.SMEM)] + [vmem] * 12,
        out_specs=(vmem,) * 5,
        scratch_shapes=[
            pltpu.VMEM(((rows + 2) * cols, 3 * ch), bf16),
            pltpu.VMEM((cells, ch), bf16),
            pltpu.VMEM((width, 2 * cells + 128), bf16),
            pltpu.VMEM((width, width + 2 * cells), bf16),
            pltpu.VMEM((width, 128), f32),
            pltpu.VMEM((width + 2 * cells + 128, TILE), bf16),
            pltpu.VMEM((width, TILE), f32),
            pltpu.VMEM((width, TILE), f32),
            pltpu.VMEM((2 * width, TILE), bf16),
            pltpu.VMEM((cells + 16, 2 * width), f32),
            pltpu.VMEM((width, 128), f32),
        ],
        compiler_params=pltpu.CompilerParams(vmem_limit_bytes=48 << 20),
        name="queries",
    )(
        base,
        queries,
        center,
        *halo,
        conv_weight.reshape(3, 3 * ch, ch),
        map_weight,
        map_bias.reshape(1, -1),
        input_weight,
        hidden_weight[0],
        output_weight.reshape(1, -1),
    )


def latent_kernel(center_ref, top_ref, bottom_ref, left_ref, right_ref, convw_ref, out_ref):
    rows, cols, ch = center_ref.shape
    cells = rows * cols
    x3 = shifted(center_ref[...], top_ref[...], bottom_ref[...], left_ref[...], right_ref[...])
    acc = None
    for a in (-1, 0, 1):
        start = (1 - a) * cols
        for b in (-1, 0, 1):
            part = dot_nt(x3[1 - b][start : start + cells], convw_ref[3 * (a + 1) + b + 1])
            acc = part if acc is None else acc + part
    out_ref[...] = acc.reshape(rows, cols, ch)


def halo_of(tile):
    lat = lax.axis_size("lat")
    lon = lax.axis_size("lon")
    up = [(i, i + 1) for i in range(lat - 1)]
    down = [(i + 1, i) for i in range(lat - 1)]
    top = lax.ppermute(tile[-1:], "lat", up)
    bottom = lax.ppermute(tile[:1], "lat", down)
    east = [(i, (i + 1) % lon) for i in range(lon)]
    west = [((i + 1) % lon, i) for i in range(lon)]

    def column(j):
        return jnp.concatenate([top[0, j : j + 1], tile[:, j], bottom[0, j : j + 1]], axis=0)

    left = lax.ppermute(column(tile.shape[1] - 1), "lon", east)
    right = lax.ppermute(column(0), "lon", west)
    return top[0], bottom[0], left, right


def on_device(
    latents,
    conv_weight,
    map_weight,
    map_bias,
    input_weight,
    hidden_weight,
    output_weight,
    hit_owner,
    serve_block,
    query_grid,
    cotangent,
):
    rows, cols, ch = latents.shape
    lat_parts = lax.axis_size("lat")
    lon_parts = lax.axis_size("lon")
    dev_count = lat_parts * lon_parts
    dims = (rows * lat_parts, cols * lon_parts)
    hits = hit_owner.shape[0]
    group = cotangent.shape[0] // hits
    f32 = jnp.float32

    grid = query_grid.reshape(3, hits, group).astype(f32)
    data = jnp.concatenate(
        [grid[0], grid[1], grid[2], cotangent.reshape(hits, group)], axis=1
    )
    pick = (
        jnp.arange(dev_count, dtype=jnp.int32)[:, None] == hit_owner[None, :]
    ).astype(f32)
    outgoing = jnp.dot(pick, data, precision=lax.Precision.HIGHEST)
    arrived = lax.all_to_all(
        outgoing.reshape(dev_count, 1, 4 * group), ("lat", "lon"), split_axis=0, concat_axis=0, tiled=True
    ).reshape(dev_count, 4, group)
    block = jnp.maximum(serve_block[0], 0).astype(f32)[:, None]
    sub = arrived[:, 1]
    sub_r = jnp.floor((sub + 0.5) * (1.0 / SUB))
    zero = jnp.zeros_like(sub)
    queries = jnp.stack(
        [
            arrived[:, 0] + BLOCK * block,
            sub_r,
            sub - SUB * sub_r,
            arrived[:, 2],
            arrived[:, 3],
            zero,
            zero,
            zero,
        ]
    ).reshape(8, dev_count * group)

    base = jnp.stack(
        [lax.axis_index("lat") * rows, lax.axis_index("lon") * cols]
    ).astype(f32)
    weights = (conv_weight, map_weight, map_bias, input_weight, hidden_weight, output_weight)
    fg, conv_part, map_part, hid_part, small = run_main(
        base, queries, latents, halo_of(latents), weights, dims
    )
    fg3 = fg.reshape(rows, cols, ch)
    vmem = pl.BlockSpec(memory_space=pltpu.VMEM)
    latent_grad = pl.pallas_call(
        latent_kernel,
        out_shape=jax.ShapeDtypeStruct((rows, cols, ch), f32),
        in_specs=[vmem] * 6,
        out_specs=vmem,
        compiler_params=pltpu.CompilerParams(vmem_limit_bytes=32 << 20),
        name="latent",
    )(fg3, *halo_of(fg3), conv_weight)
    conv_part, map_part, hid_part, small = lax.psum(
        (conv_part, map_part, hid_part, small), ("lat", "lon")
    )
    scale = float(hits * group * dev_count) ** (-0.5)
    width = input_weight.shape[1]
    small = small * scale
    return (
        latent_grad,
        conv_part.reshape(9, ch, ch) * scale,
        map_part * scale,
        small[0],
        jnp.stack([small[1, :width], small[1, width:], small[2, :width]]),
        hid_part[None] * scale,
        small[2, width:],
    )


def solution(mesh):
    placed = (
        P("lat", "lon", None),
        P(),
        P(),
        P(),
        P(),
        P(),
        P(),
        P(("lat", "lon")),
        P(("lat", "lon"), None),
        P(None, ("lat", "lon")),
        P(("lat", "lon")),
    )
    return jax.shard_map(
        on_device,
        mesh=mesh,
        in_specs=placed,
        out_specs=(P("lat", "lon", None), P(), P(), P(), P(), P(), P()),
        check_vma=False,
    )
```

time: 1210 us -> 268 us (0.22)
  matrix products: 324 us -> 0.95 us
  blocking collectives: 297 us -> 64.2 us
  local copies, waits for them, and re-layouts: 201 us -> 6.32 us
  waiting for transfers between devices: 242 us -> 80.3 us
  Pallas kernels: 0 us -> 61.5 us
  other arithmetic: 63 us -> 7.95 us
  starting transfers between devices: 45.4 us -> 32 us
  loops' own time: 13 us -> 0 us
    dot_general x162 -> x1, matrix products: 324 us -> 0.95 us  [on_device(): outgoing = jnp.dot(pick, data, precision=lax.Precision.HIGHEST)]
    psum x1, blocking collectives: 297 us -> 64.2 us  [on_device(): lax.psum((conv_part, map_part, hid_part, small), ('lat', 'lon'))]
    all_to_all x3 -> x1, waiting for transfers between devices: 92.8 us -> 3.3 us  [on_device(): lax.all_to_all(outgoing.reshape(dev_count, 1, 4 * group), ('lat', 'lon'),...]
    psum x1, waiting for transfers between devices: 148 us -> 77 us  [on_device(): lax.psum((conv_part, map_part, hid_part, small), ('lat', 'lon'))]
    pallas_call x0 -> x2, Pallas kernels: none -> 61.5 us  [the longest x1 60.3 us: run_main(): pl.pallas_call(functools.partial(main_kernel, dims), out_shape=(jax.Shape...]
    add x84 -> x2, local copies, waits for them, and re-layouts: 40.6 us -> 0.19 us  [on_device(): arrived[:, 0] + BLOCK * block]
    sub x36 -> x1, other arithmetic: 33.4 us -> 0.06 us  [on_device(): sub - SUB * sub_r]
    unnamed x46 -> x22, local copies, waits for them, and re-layouts: 25.7 us -> 0.06 us
  transfers between devices with their start and end apart: 12 -> 10, of which waited for: 4 -> 2; matrix products, arithmetic and copies ran while one was open for 3% -> 3% of each run, Pallas kernels for 0% -> 0%
where the time goes in v1:
time: 268 us
  waiting for transfers between devices  80.3 us (30%)
  blocking collectives  64.2 us (24%)
  Pallas kernels  61.5 us (23%)
  starting transfers between devices  32 us (12%)
  between operations  14.4 us (5%)
  other arithmetic  7.95 us (3%)
  local copies, waits for them, and re-layouts  6.32 us (2%)
    psum x1, waiting for transfers between devices, on_device(): lax.psum((conv_part, map_part, hid_part, small), ('lat', 'lon'))  77 us
    psum x1, blocking collectives, on_device(): lax.psum((conv_part, map_part, hid_part, small), ('lat', 'lon'))  64.2 us
    pallas_call x1, Pallas kernels, run_main(): pl.pallas_call(functools.partial(main_kernel, dims), out_shape=(jax.Shape...  60.3 us
    all_to_all x1, starting transfers between devices, on_device(): lax.all_to_all(outgoing.reshape(dev_count, 1, 4 * group), ('lat', 'lon'),...  9.65 us
    ppermute x2, starting transfers between devices, halo_of(): right = lax.ppermute(column(0), 'lon', west)  8.31 us
    ppermute x2, starting transfers between devices, halo_of(): top = lax.ppermute(tile[-1:], 'lat', up)  6.51 us
    ppermute x2, starting transfers between devices, halo_of(): bottom = lax.ppermute(tile[:1], 'lat', down)  5.89 us
  transfers between devices with their start and end apart: 10, of which 2 were waited for; matrix products, arithmetic and copies ran while one was open for 3% of the time, Pallas kernels for 0%

profile of v1, /device:TPU:1, one launch (start us, length us, event | category | flops | bytes accessed | tf_op | source)
XLA Modules:
  0.0 267.7 jit_solution(10911939728427216113)
XLA Ops:
  7.2 0.9 fusion.11
  8.1 3.3 %collective-permute-start.1 = (bf16[1,16,256]{2,1,0:T(8,128)(2,1)S(1)}, bf16[1,16,256]{2,1,0:T(8,128)(2,1)S(1)}, u32[]{:S(2)}, u32[]{:S(2)}) collective-permute-start(bf16[1,16,256]{2,1,0:T(8,128)(2,1)S(1)} %get-tuple-element.29), channel_id=1, source_target_pairs={{16,0},{32,16},{48,32},{64,48},{80,64},{96,80},{112,96},{17,1},{33... | collective-permute-start | bytes 24584 | tf_op jit(solution)/shard_map/ppermute | solution.py:315
  11.4 3.5 %collective-permute-start = (bf16[1,16,256]{2,1,0:T(8,128)(2,1)S(1)}, bf16[1,16,256]{2,1,0:T(8,128)(2,1)S(1)}, u32[]{:S(2)}, u32[]{:S(2)}) collective-permute-start(bf16[1,16,256]{2,1,0:T(8,128)(2,1)S(1)} %get-tuple-element.30), channel_id=1, source_target_pairs={{0,16},{16,32},{32,48},{48,64},{64,80},{80,96},{96,112},{1,17},{17... | collective-permute-start | bytes 24584 | tf_op jit(solution)/shard_map/ppermute | solution.py:314
  15.0 0.8 reshape.133
  15.8 0.9 convert_element_type.17
  17.1 1.0 convolution_bitcast_fusion
  18.1 0.8 copy.34
  18.9 9.7 %all-to-all-start = ((f32[128,1,256]{2,1,0:T(1,128)}), f32[128,1,256]{2,1,0:T(1,128)S(1)}, u32[]{:S(2)}, u32[]{:S(2)}) async-start(f32[128,1,256]{2,1,0:T(1,128)} %copy.34), calls=%async_computation | async-start | bytes 262144 | tf_op jit(solution)/shard_map/all_to_all | solution.py:357
  28.6 0.9 fusion.10
  29.5 0.7 multiply_bitcast_fusion.1
  30.3 1.5 collective-permute-start.2
  31.8 3.5 %collective-permute-start.3 = (bf16[18,256]{1,0:T(8,128)(2,1)S(1)}, bf16[18,256]{1,0:T(8,128)(2,1)S(1)}, u32[]{:S(2)}, u32[]{:S(2)}) collective-permute-start(bf16[18,256]{1,0:T(8,128)(2,1)S(1)} %pad_maximum_fusion.1), channel_id=1, source_target_pairs={{1,0},{2,1},{3,2},{4,3},{5,4},{6,5},{7,6},{8,7},{9,8},{10,9},{11,1... | collective-permute-start | bytes 27656 | tf_op jit(solution)/shard_map/ppermute | solution.py:323
  35.3 3.3 %all-to-all-done = f32[128,1,256]{2,1,0:T(1,128)S(1)} async-done(((f32[128,1,256]{2,1,0:T(1,128)}), f32[128,1,256]{2,1,0:T(1,128)S(1)}, u32[]{:S(2)}, u32[]{:S(2)}) %all-to-all-start) | async-done | bytes 131104 | tf_op jit(solution)/shard_map/all_to_all | solution.py:357
  40.1 60.3 %queries.1 = (bf16[256,256]{1,0:T(8,128)(2,1)S(1)}, f32[3,768,256]{2,1,0:T(8,128)}, f32[256,1024]{1,0:T(8,128)}, f32[512,512]{1,0:T(8,128)}, f32[3,1024]{1,0:T(4,128)S(1)}) custom-call(f32[2]{0:T(128)S(1)} %add_convert_fusion.base_ref, f32[8,8192]{1,0:T(8,128)S(1)} %stack.31.q_ref, bf16[16,16,256]{2,1,0:T(8,128)(2,1)S(1)} %copy-done.3, ...), custom_call_target="tpu_custom_call" | custom-call | tf_op jit(solution)/shard_map/queries/pallas_call | solution.py:256
  100.4 2.6 collective-permute-start.5
  103.0 3.0 %collective-permute-start.4 = (bf16[1,16,256]{2,1,0:T(8,128)(2,1)S(1)}, bf16[1,16,256]{2,1,0:T(8,128)(2,1)S(1)}, u32[]{:S(2)}, u32[]{:S(2)}) collective-permute-start(bf16[1,16,256]{2,1,0:T(8,128)(2,1)S(1)} %get-tuple-element.26), channel_id=1, source_target_pairs={{0,16},{16,32},{32,48},{48,64},{64,80},{80,96},{96,112},{1,17},{17... | collective-permute-start | bytes 24584 | tf_op jit(solution)/shard_map/ppermute | solution.py:314
  106.0 64.2 %psum.30 = f32[3,1024]{1,0:T(4,128)S(1)} all-reduce(f32[3,1024]{1,0:T(4,128)S(1)} %get-tuple-element.15), channel_id=1, replica_groups=mesh['lat'=8,'lon'=16] {'lat','lon'}, use_global_device_ids=true, to_apply=%region_2.0 | all-reduce | flops 3072 | bytes 24576 | tf_op jit(solution)/shard_map/psum | solution.py:394
  171.1 4.8 %collective-permute-start.7 = (bf16[18,256]{1,0:T(8,128)(2,1)S(1)}, bf16[18,256]{1,0:T(8,128)(2,1)S(1)}, u32[]{:S(2)}, u32[]{:S(2)}) collective-permute-start(bf16[18,256]{1,0:T(8,128)(2,1)S(1)} %pad_maximum_fusion.3), channel_id=1, source_target_pairs={{1,0},{2,1},{3,2},{4,3},{5,4},{6,5},{7,6},{8,7},{9,8},{10,9},{11,1... | collective-permute-start | bytes 27656 | tf_op jit(solution)/shard_map/ppermute | solution.py:323
  175.9 0.6 pad_maximum_fusion.4
  177.1 1.2 latent.1
  178.3 77.0 %all-reduce.3.cloned.1.call-done = (f32[3,768,256]{2,1,0:T(8,128)}, f32[256,1024]{1,0:T(8,128)}, f32[512,512]{1,0:T(8,128)}) async-done(((f32[3,768,256]{2,1,0:T(8,128)}, f32[256,1024]{1,0:T(8,128)}, f32[512,512]{1,0:T(8,128)}), (f32[3,768,256]{2,1,0:T(8,128)}, f32[256,1024]{1,0:T(8,128)}, f32[512,512]{1,0:T(8,128)})) %all-reduce.3.cloned.1.call-update) | async-done | bytes 4456464 | tf_op jit(solution)/shard_map/psum | solution.py:394
  255.3 3.4 %broadcast_multiply_fusion = f32[3,768,256]{2,1,0:T(8,128)} fusion(f32[3,768,256]{2,1,0:T(8,128)} %get-tuple-element.20), kind=kLoop, calls=%fused_computation | loop fusion | flops 589824 | bytes 4718592 | tf_op jit(solution)/shard_map/mul | solution.py:402
  258.7 1.1 broadcast_multiply_fusion.1
  259.8 1.1 multiply_bitcast_fusion
  (65 shorter events, 3.4 us)
Async XLA Ops:
  7.2 32.9 %copy-start.3 = (bf16[16,16,256]{2,1,0:T(8,128)(2,1)S(1)}, bf16[16,16,256]{2,1,0:T(8,128)(2,1)}, u32[]{:S(2)}) copy-start(bf16[16,16,256]{2,1,0:T(8,128)(2,1)} %center_ref.1) | copy-start | bytes 393220
  7.2 32.9 %copy-start = (bf16[9,256,256]{2,1,0:T(8,128)(2,1)S(1)}, bf16[9,256,256]{2,1,0:T(8,128)(2,1)}, u32[]{:S(2)}) copy-start(bf16[9,256,256]{2,1,0:T(8,128)(2,1)} %convw_ref.1) | copy-start | bytes 3538948
  7.2 32.9 %copy-start.6 = (f32[512]{0:T(512)S(1)}, f32[512]{0:T(512)}, u32[]{:S(2)}) copy-start(f32[512]{0:T(512)} %param.17) | copy-start | bytes 6148
  7.2 32.9 %copy-start.2 = (bf16[1,512,512]{2,1,0:T(8,128)(2,1)S(1)}, bf16[1,512,512]{2,1,0:T(8,128)(2,1)}, u32[]{:S(2)}) copy-start(bf16[1,512,512]{2,1,0:T(8,128)(2,1)} %param.16) | copy-start | bytes 1572868
  7.2 32.9 %copy-start.4 = (f32[3,512]{1,0:T(4,128)S(1)}, f32[3,512]{1,0:T(4,128)}, u32[]{:S(2)}) copy-start(f32[3,512]{1,0:T(4,128)} %inw_ref.1) | copy-start | bytes 18436
  7.2 32.9 %copy-start.5 = (f32[1024]{0:T(1024)S(1)}, f32[1024]{0:T(1024)}, u32[]{:S(2)}) copy-start(f32[1024]{0:T(1024)} %param.14) | copy-start | bytes 12292
  7.2 32.9 %copy-start.1 = (bf16[256,1024]{1,0:T(8,128)(2,1)S(1)}, bf16[256,1024]{1,0:T(8,128)(2,1)}, u32[]{:S(2)}) copy-start(bf16[256,1024]{1,0:T(8,128)(2,1)} %mapw_ref.1) | copy-start | bytes 1572868
  8.1 22.1 %collective-permute-start.1 = (bf16[1,16,256]{2,1,0:T(8,128)(2,1)S(1)}, bf16[1,16,256]{2,1,0:T(8,128)(2,1)S(1)}, u32[]{:S(2)}, u32[]{:S(2)}) collective-permute-start(bf16[1,16,256]{2,1,0:T(8,128)(2,1)S(1)} %get-tuple-element.29), channel_id=1, source_target_pairs={{16,0},{32,16},{48,32},{64,48},{80,64},{96,80},{112,96},{17,1},{33... | collective-permute-start | bytes 24584 | tf_op jit(solution)/shard_map/ppermute | solution.py:315
  11.4 18.8 %collective-permute-start = (bf16[1,16,256]{2,1,0:T(8,128)(2,1)S(1)}, bf16[1,16,256]{2,1,0:T(8,128)(2,1)S(1)}, u32[]{:S(2)}, u32[]{:S(2)}) collective-permute-start(bf16[1,16,256]{2,1,0:T(8,128)(2,1)S(1)} %get-tuple-element.30), channel_id=1, source_target_pairs={{0,16},{16,32},{32,48},{48,64},{64,80},{80,96},{96,112},{1,17},{17... | collective-permute-start | bytes 24584 | tf_op jit(solution)/shard_map/ppermute | solution.py:314
  18.9 19.7 %all-to-all-start = ((f32[128,1,256]{2,1,0:T(1,128)}), f32[128,1,256]{2,1,0:T(1,128)S(1)}, u32[]{:S(2)}, u32[]{:S(2)}) async-start(f32[128,1,256]{2,1,0:T(1,128)} %copy.34), calls=%async_computation | async-start | bytes 262144 | tf_op jit(solution)/shard_map/all_to_all | solution.py:357
  28.5 226.8 %all-reduce.3.cloned.1.call-start = ((), (), s32[]{:S(2)}) async-start(), calls=%async_computation.1 | async-start | bytes 8912896 | tf_op jit(solution)/shard_map/psum | solution.py:394
  30.3 9.7 %collective-permute-start.2 = (bf16[18,256]{1,0:T(8,128)(2,1)S(1)}, bf16[18,256]{1,0:T(8,128)(2,1)S(1)}, u32[]{:S(2)}, u32[]{:S(2)}) collective-permute-start(bf16[18,256]{1,0:T(8,128)(2,1)S(1)} %pad_maximum_fusion), channel_id=1, source_target_pairs={{0,1},{1,2},{2,3},{3,4},{4,5},{5,6},{6,7},{7,8},{8,9},{9,10},{10,1... | collective-permute-start | bytes 27656 | tf_op jit(solution)/shard_map/ppermute | solution.py:322
  31.8 8.2 %collective-permute-start.3 = (bf16[18,256]{1,0:T(8,128)(2,1)S(1)}, bf16[18,256]{1,0:T(8,128)(2,1)S(1)}, u32[]{:S(2)}, u32[]{:S(2)}) collective-permute-start(bf16[18,256]{1,0:T(8,128)(2,1)S(1)} %pad_maximum_fusion.1), channel_id=1, source_target_pairs={{1,0},{2,1},{3,2},{4,3},{5,4},{6,5},{7,6},{8,7},{9,8},{10,9},{11,1... | collective-permute-start | bytes 27656 | tf_op jit(solution)/shard_map/ppermute | solution.py:323
  100.4 70.5 %collective-permute-start.5 = (bf16[1,16,256]{2,1,0:T(8,128)(2,1)S(1)}, bf16[1,16,256]{2,1,0:T(8,128)(2,1)S(1)}, u32[]{:S(2)}, u32[]{:S(2)}) collective-permute-start(bf16[1,16,256]{2,1,0:T(8,128)(2,1)S(1)} %get-tuple-element.25), channel_id=1, source_target_pairs={{16,0},{32,16},{48,32},{64,48},{80,64},{96,80},{112,96},{17,1},{33... | collective-permute-start | bytes 24584 | tf_op jit(solution)/shard_map/ppermute | solution.py:315
  103.0 67.9 %collective-permute-start.4 = (bf16[1,16,256]{2,1,0:T(8,128)(2,1)S(1)}, bf16[1,16,256]{2,1,0:T(8,128)(2,1)S(1)}, u32[]{:S(2)}, u32[]{:S(2)}) collective-permute-start(bf16[1,16,256]{2,1,0:T(8,128)(2,1)S(1)} %get-tuple-element.26), channel_id=1, source_target_pairs={{0,16},{16,32},{32,48},{48,64},{64,80},{80,96},{96,112},{1,17},{17... | collective-permute-start | bytes 24584 | tf_op jit(solution)/shard_map/ppermute | solution.py:314
  170.9 6.1 %collective-permute-start.6 = (bf16[18,256]{1,0:T(8,128)(2,1)S(1)}, bf16[18,256]{1,0:T(8,128)(2,1)S(1)}, u32[]{:S(2)}, u32[]{:S(2)}) collective-permute-start(bf16[18,256]{1,0:T(8,128)(2,1)S(1)} %pad_maximum_fusion.2), channel_id=1, source_target_pairs={{0,1},{1,2},{2,3},{3,4},{4,5},{5,6},{6,7},{7,8},{8,9},{9,10},{10,1... | collective-permute-start | bytes 27656 | tf_op jit(solution)/shard_map/ppermute | solution.py:322
  171.1 6.0 %collective-permute-start.7 = (bf16[18,256]{1,0:T(8,128)(2,1)S(1)}, bf16[18,256]{1,0:T(8,128)(2,1)S(1)}, u32[]{:S(2)}, u32[]{:S(2)}) collective-permute-start(bf16[18,256]{1,0:T(8,128)(2,1)S(1)} %pad_maximum_fusion.3), channel_id=1, source_target_pairs={{1,0},{2,1},{3,2},{4,3},{5,4},{6,5},{7,6},{8,7},{9,8},{10,9},{11,1... | collective-permute-start | bytes 27656 | tf_op jit(solution)/shard_map/ppermute | solution.py:323
  255.3 3.4 %copy-start.8 = (f32[256,1024]{1,0:T(8,128)S(1)}, f32[256,1024]{1,0:T(8,128)}, u32[]{:S(2)}) copy-start(f32[256,1024]{1,0:T(8,128)} %get-tuple-element.21) | copy-start | bytes 3145732
  255.3 4.5 %copy-start.7 = (f32[512,512]{1,0:T(8,128)S(1)}, f32[512,512]{1,0:T(8,128)}, u32[]{:S(2)}) copy-start(f32[512,512]{1,0:T(8,128)} %get-tuple-element.22) | copy-start | bytes 3145732
Sparse Core Ops, SparseCore 0:
  100.5 154.7 all-reduce.2

commit v2 on v1

--- a/solution.py
+++ b/solution.py
@@ -100,10 +100,9 @@
     hid_ref,
     outw_ref,
     fg_ref,
-    conv_ref,
-    map_ref,
+    grads_ref,
+    small_ref,
     hidg_ref,
-    small_ref,
     x3_ref,
     feat_ref,
     tab0_ref,
@@ -225,9 +224,15 @@
     fg = (dot_nt(hi, mapw_ref[...]) + dot_nt(lo, mapw_ref[...])).astype(bf16)
     fg_ref[...] = fg
     feat_t = feat_ref[...].astype(f32).T.astype(bf16)
-    map_ref[...] = dot(feat_t, hi) + dot(feat_t, lo)
+    grad = dot(feat_t, hi) + dot(feat_t, lo)
+    for k in range(4):
+        grads_ref[9 + k] = grad[:, k * ch : (k + 1) * ch]
+        r, c = k // 2 * ch, k % 2 * ch
+        grads_ref[13 + k] = hidg_ref[r : r + ch, c : c + ch]
     for a in range(3):
-        conv_ref[a] = dot_tn(x3_ref[a * cols : a * cols + cells, :], fg)
+        grad = dot_tn(x3_ref[a * cols : a * cols + cells, :], fg)
+        for b in range(3):
+            grads_ref[3 * a + b] = grad[b * ch : (b + 1) * ch, :]
     bias = jnp.sum(g, axis=0, keepdims=True)
     g0 = g[:, :width]
     ig0 = jnp.sum(lat_c * g0, axis=0, keepdims=True) + (2.0 / (lat_cells * SUB)) * g_ref[
@@ -238,6 +243,7 @@
     ]
     ig2 = lev_c * bias[:, :width] + (2.0 / LEVELS) * g_ref[cells + 2 : cells + 3, :width]
     og = jnp.sum(og_ref[...].T, axis=0, keepdims=True)
+    small_ref[...] = jnp.zeros_like(small_ref)
     small_ref[0:1, :] = bias
     small_ref[1:2, 0:width] = OMEGA * ig0
     small_ref[1:2, width:] = OMEGA * ig1
@@ -257,14 +263,13 @@
         functools.partial(main_kernel, dims),
         out_shape=(
             jax.ShapeDtypeStruct((cells, ch), bf16),
-            jax.ShapeDtypeStruct((3, 3 * ch, ch), f32),
-            jax.ShapeDtypeStruct((ch, 2 * width), f32),
-            jax.ShapeDtypeStruct((width, width), f32),
-            jax.ShapeDtypeStruct((3, 2 * width), f32),
+            jax.ShapeDtypeStruct((17, ch, ch), f32),
+            jax.ShapeDtypeStruct((8, 2 * width), f32),
         ),
         in_specs=[pl.BlockSpec(memory_space=pltpu.SMEM)] + [vmem] * 12,
-        out_specs=(vmem,) * 5,
+        out_specs=(vmem,) * 3,
         scratch_shapes=[
+            pltpu.VMEM((width, width), f32),
             pltpu.VMEM(((rows + 2) * cols, 3 * ch), bf16),
             pltpu.VMEM((cells, ch), bf16),
             pltpu.VMEM((width, 2 * cells + 128), bf16),
@@ -293,17 +298,355 @@
     )
 
 
-def latent_kernel(center_ref, top_ref, bottom_ref, left_ref, right_ref, convw_ref, out_ref):
-    rows, cols, ch = center_ref.shape
-    cells = rows * cols
-    x3 = shifted(center_ref[...], top_ref[...], bottom_ref[...], left_ref[...], right_ref[...])
+def finish_kernel(
+    sizes,
+    scale,
+    fg_ref,
+    convw_ref,
+    wg_ref,
+    small_ref,
+    latent_ref,
+    conv_ref,
+    map_ref,
+    hid_ref,
+    total_ref,
+    send1,
+    recv1,
+    acc1,
+    send2,
+    recv2,
+    acc2,
+    send3,
+    recv3,
+    slots4,
+    half,
+    other,
+    pair_s,
+    x_s,
+    y_s,
+    z_s,
+    row_s,
+    row_r,
+    col_s,
+    col_r,
+    sem_s,
+    sem_r,
+    ssem_s,
+    ssem_r,
+    hsem_s,
+    hsem_r,
+):
+    nx, ny, nz = sizes
+    bf16 = jnp.bfloat16
+    f32 = jnp.float32
+    lat = lax.axis_index("lat")
+    lon = lax.axis_index("lon")
+    lat_n = lax.axis_size("lat")
+    lon_n = lax.axis_size("lon")
+    z, c = lax.div(lat, 2), lax.rem(lat, 2)
+    x, y = lax.div(lon, ny), lax.rem(lon, ny)
+    blocks, rows, lanes = half.shape
+    quarter = rows // nx
+    final = quarter // ny
+
+    def at_pair():
+        return (lat + 1 - 2 * c, lon)
+
+    def at_x(d):
+        return (lat, lax.rem(x + d, nx) * ny + y)
+
+    def at_y(d):
+        return (lat, x * ny + lax.rem(y + d, ny))
+
+    def at_z(d):
+        return (lax.rem(z + d, nz) * 2 + c, lon)
+
+    def at_first(d):
+        return (lat, (1 - c) * (lax.rem(x + d, nx) * ny + y) + c * (x * ny + lax.rem(y + d, ny)))
+
+    def at_second(d):
+        return (lat, c * (lax.rem(x + d, nx) * ny + y) + (1 - c) * (x * ny + lax.rem(y + d, ny)))
+
+    first = (1 - c) * x + c * y
+    second = c * x + (1 - c) * y
+
+    def copy(src, dst, s, r, device):
+        return pltpu.make_async_remote_copy(
+            src_ref=src,
+            dst_ref=dst,
+            send_sem=s,
+            recv_sem=r,
+            device_id=device,
+            device_id_type=pl.DeviceIdType.MESH,
+        )
+
+    around = [(-1, 0), (1, 0), (0, -1), (0, 1), (-1, -1), (-1, 1), (1, -1), (1, 1)]
+
+    def at_rim(da, db):
+        return (lax.rem(lat + da + lat_n, lat_n), lax.rem(lon + db + lon_n, lon_n))
+
+    barrier = pltpu.get_barrier_semaphore()
+    peers = [at_pair()]
+    peers += [at_x(d) for d in range(1, nx)]
+    peers += [at_y(d) for d in range(1, ny)]
+    peers += [at_z(d) for d in range(1, nz)]
+    peers += [at_rim(da, db) for da, db in around]
+    for peer in peers:
+        pl.semaphore_signal(barrier, inc=1, device_id=peer, device_id_type=pl.DeviceIdType.MESH)
+
+    tile_rows, cols, ch = latent_ref.shape
+    keep = pl.ds(pl.multiple_of(c * lanes, lanes), lanes)
+    give = pl.ds(pl.multiple_of((1 - c) * lanes, lanes), lanes)
+
+    def to_send1(b, carry):
+        send1[b] = wg_ref[b, :, give].astype(bf16)
+        return carry
+
+    lax.fori_loop(0, blocks, to_send1, 0)
+    fg = fg_ref[...]
+    fg32 = fg.astype(f32).reshape(tile_rows, cols, ch)
+    col_s[0] = fg32[:, cols - 1, :].astype(bf16)
+    col_s[1] = fg32[:, 0, :].astype(bf16)
+    pair_s[c] = small_ref[...]
+
+    pl.semaphore_wait(barrier, len(peers))
+
+    cells = tile_rows * cols
+    rim = [
+        copy(fg_ref.at[pl.ds(0, cols)], row_r.at[1], hsem_s.at[0], hsem_r.at[1], at_rim(-1, 0)),
+        copy(fg_ref.at[pl.ds(cells - cols, cols)], row_r.at[0], hsem_s.at[1], hsem_r.at[0], at_rim(1, 0)),
+        copy(col_s.at[0], col_r.at[0], hsem_s.at[2], hsem_r.at[2], at_rim(0, 1)),
+        copy(col_s.at[1], col_r.at[1], hsem_s.at[3], hsem_r.at[3], at_rim(0, -1)),
+        copy(fg_ref.at[pl.ds(cells - cols, cols)], row_r.at[2], hsem_s.at[4], hsem_r.at[4], at_rim(1, 1)),
+        copy(fg_ref.at[pl.ds(cells - cols, cols)], row_r.at[3], hsem_s.at[5], hsem_r.at[5], at_rim(1, -1)),
+        copy(fg_ref.at[pl.ds(0, cols)], row_r.at[4], hsem_s.at[6], hsem_r.at[6], at_rim(-1, 1)),
+        copy(fg_ref.at[pl.ds(0, cols)], row_r.at[5], hsem_s.at[7], hsem_r.at[7], at_rim(-1, -1)),
+    ]
+    p1 = copy(send1, recv1, sem_s.at[0], sem_r.at[0], at_pair())
+    p1.start()
+    q1 = copy(pair_s.at[c], pair_s.at[c], ssem_s.at[0], ssem_r.at[0], at_pair())
+    q1.start()
+    for item in rim:
+        item.start()
+
+    q1.wait()
+    x_s[x] = pair_s[0] + pair_s[1]
+    q2 = [
+        copy(x_s.at[x], x_s.at[x], ssem_s.at[d], ssem_r.at[d], at_x(d)) for d in range(1, nx)
+    ]
+    for item in q2:
+        item.start()
+
+    p1.wait()
+
+    def add1(b, carry):
+        v = wg_ref[b, :, keep] + recv1[b].astype(f32)
+        acc1[b] = v
+        send2[b] = v.astype(bf16)
+        return carry
+
+    lax.fori_loop(0, blocks, add1, 0)
+    p2 = []
+    for d in range(1, nx):
+        target = lax.rem(first + d, nx)
+        p2.append(
+            copy(
+                send2.at[:, pl.ds(pl.multiple_of(target * quarter, quarter), quarter), :],
+                recv2.at[d - 1],
+                sem_s.at[d],
+                sem_r.at[d],
+                at_first(d),
+            )
+        )
+        p2[-1].start()
+    for item in q2:
+        item.wait()
+    y_s[y] = (x_s[0] + x_s[1]) + (x_s[2] + x_s[3])
+    q3 = [
+        copy(y_s.at[y], y_s.at[y], ssem_s.at[3 + d], ssem_r.at[3 + d], at_y(d))
+        for d in range(1, ny)
+    ]
+    for item in q3:
+        item.start()
+
+    for item in rim:
+        item.wait()
+    up_ok = jnp.where(lat > 0, 1.0, 0.0).astype(f32)
+    down_ok = jnp.where(lat < lat_n - 1, 1.0, 0.0).astype(f32)
+    top = (row_r[0].astype(f32) * up_ok).astype(bf16)
+    bottom = (row_r[1].astype(f32) * down_ok).astype(bf16)
+    nw = row_r[2].astype(f32)[cols - 1 : cols] * up_ok
+    ne = row_r[3].astype(f32)[0:1] * up_ok
+    sw = row_r[4].astype(f32)[cols - 1 : cols] * down_ok
+    se = row_r[5].astype(f32)[0:1] * down_ok
+    left = jnp.concatenate([nw, col_r[0].astype(f32), sw], axis=0)
+    right = jnp.concatenate([ne, col_r[1].astype(f32), se], axis=0)
+    x3 = shifted(fg.reshape(tile_rows, cols, ch), top, bottom, left, right)
     acc = None
     for a in (-1, 0, 1):
         start = (1 - a) * cols
         for b in (-1, 0, 1):
             part = dot_nt(x3[1 - b][start : start + cells], convw_ref[3 * (a + 1) + b + 1])
             acc = part if acc is None else acc + part
-    out_ref[...] = acc.reshape(rows, cols, ch)
+    latent_ref[...] = acc.reshape(tile_rows, cols, ch)
+
+    for item in p2:
+        item.wait()
+    mine = pl.ds(pl.multiple_of(first * quarter, quarter), quarter)
+
+    def add2(b, carry):
+        v = acc1[b, mine, :]
+        for d in range(nx - 1):
+            v += recv2[d, b].astype(f32)
+        acc2[b] = v
+        send3[b] = v.astype(bf16)
+        return carry
+
+    lax.fori_loop(0, blocks, add2, 0)
+    p3 = []
+    for d in range(1, ny):
+        target = lax.rem(second + d, ny)
+        p3.append(
+            copy(
+                send3.at[:, pl.ds(pl.multiple_of(target * final, final), final), :],
+                recv3.at[d - 1],
+                sem_s.at[3 + d],
+                sem_r.at[3 + d],
+                at_second(d),
+            )
+        )
+        p3[-1].start()
+    for item in q3:
+        item.wait()
+    z_s[z] = (y_s[0] + y_s[1]) + (y_s[2] + y_s[3])
+    q4 = [
+        copy(z_s.at[z], z_s.at[z], ssem_s.at[6 + d], ssem_r.at[6 + d], at_z(d))
+        for d in range(1, nz)
+    ]
+    for item in q4:
+        item.start()
+    for item in p3:
+        item.wait()
+    ours = pl.ds(pl.multiple_of(second * final, final), final)
+
+    def add3(b, carry):
+        v = acc2[b, ours, :]
+        for d in range(ny - 1):
+            v += recv3[d, b].astype(f32)
+        slots4[z, b] = v.astype(bf16)
+        return carry
+
+    lax.fori_loop(0, blocks, add3, 0)
+    p4 = [
+        copy(slots4.at[z], slots4.at[z], sem_s.at[6 + d], sem_r.at[6 + d], at_z(d))
+        for d in range(1, nz)
+    ]
+    for item in p4:
+        item.start()
+    for item in q4:
+        item.wait()
+    total_ref[...] = ((z_s[0] + z_s[1]) + (z_s[2] + z_s[3])) * scale
+    for item in p4:
+        item.wait()
+    place = pl.ds(pl.multiple_of(first * quarter + second * final, final), final)
+
+    def add4(b, carry):
+        v = (slots4[0, b].astype(f32) + slots4[1, b].astype(f32)) + (
+            slots4[2, b].astype(f32) + slots4[3, b].astype(f32)
+        )
+        half[b, place, :] = v.astype(bf16)
+        return carry
+
+    lax.fori_loop(0, blocks, add4, 0)
+    p5 = [
+        copy(half.at[:, place, :], half.at[:, place, :], sem_s.at[9 + d], sem_r.at[9 + d], at_second(d))
+        for d in range(1, ny)
+    ]
+    for item in p5:
+        item.start()
+    for item in p5:
+        item.wait()
+    p6 = [
+        copy(half.at[:, mine, :], half.at[:, mine, :], sem_s.at[12 + d], sem_r.at[12 + d], at_first(d))
+        for d in range(1, nx)
+    ]
+    for item in p6:
+        item.start()
+    for item in p6:
+        item.wait()
+    p7 = copy(half, other, sem_s.at[16], sem_r.at[16], at_pair())
+    p7.start()
+
+    def write(source, core):
+        def conv_out(b, carry):
+            lane = pl.ds(pl.multiple_of(core * lanes, lanes), lanes)
+            conv_ref[b, :, lane] = source[b].astype(f32) * scale
+            return carry
+
+        lax.fori_loop(0, 9, conv_out, 0)
+        for k in range(4):
+            lane = pl.ds(pl.multiple_of(k * rows + core * lanes, lanes), lanes)
+            map_ref[:, lane] = source[9 + k].astype(f32) * scale
+            lane = pl.ds(pl.multiple_of(k % 2 * rows + core * lanes, lanes), lanes)
+            hid_ref[k // 2 * rows : (k // 2 + 1) * rows, lane] = source[13 + k].astype(f32) * scale
+
+    write(half, c)
+    p7.wait()
+    write(other, 1 - c)
+
+
+def run_finish(fg, conv_weight, grads, small, tile_shape, scale, width):
+    rows, cols, ch = tile_shape
+    f32 = jnp.float32
+    bf16 = jnp.bfloat16
+    blocks, size, _ = grads.shape
+    lanes = size // 2
+    nx, ny, nz = 4, 4, 4
+    dma = pltpu.SemaphoreType.DMA
+    vmem = pl.BlockSpec(memory_space=pltpu.VMEM)
+    return pl.pallas_call(
+        functools.partial(finish_kernel, (nx, ny, nz), scale),
+        out_shape=(
+            jax.ShapeDtypeStruct((rows, cols, ch), f32),
+            jax.ShapeDtypeStruct((9, ch, ch), f32),
+            jax.ShapeDtypeStruct((ch, 2 * width), f32),
+            jax.ShapeDtypeStruct((width, width), f32),
+            jax.ShapeDtypeStruct(small.shape, f32),
+        ),
+        in_specs=[vmem] * 4,
+        out_specs=(vmem,) * 5,
+        scratch_shapes=[
+            pltpu.VMEM((blocks, size, lanes), bf16),
+            pltpu.VMEM((blocks, size, lanes), bf16),
+            pltpu.VMEM((blocks, size, lanes), f32),
+            pltpu.VMEM((blocks, size, lanes), bf16),
+            pltpu.VMEM((nx - 1, blocks, size // nx, lanes), bf16),
+            pltpu.VMEM((blocks, size // nx, lanes), f32),
+            pltpu.VMEM((blocks, size // nx, lanes), bf16),
+            pltpu.VMEM((ny - 1, blocks, size // nx // ny, lanes), bf16),
+            pltpu.VMEM((nz, blocks, size // nx // ny, lanes), bf16),
+            pltpu.VMEM((blocks, size, lanes), bf16),
+            pltpu.VMEM((blocks, size, lanes), bf16),
+            pltpu.VMEM((2,) + small.shape, f32),
+            pltpu.VMEM((nx,) + small.shape, f32),
+            pltpu.VMEM((ny,) + small.shape, f32),
+            pltpu.VMEM((nz,) + small.shape, f32),
+            pltpu.VMEM((1, cols, ch), bf16),
+            pltpu.VMEM((6, cols, ch), bf16),
+            pltpu.VMEM((2, rows, ch), bf16),
+            pltpu.VMEM((2, rows, ch), bf16),
+            dma((17,)),
+            dma((17,)),
+            dma((10,)),
+            dma((10,)),
+            dma((8,)),
+            dma((8,)),
+        ],
+        compiler_params=pltpu.CompilerParams(
+            vmem_limit_bytes=48 << 20, collective_id=1, has_side_effects=True
+        ),
+        name="finish",
+    )(fg, conv_weight, grads, small)
 
 
 def halo_of(tile):
@@ -378,32 +721,19 @@
         [lax.axis_index("lat") * rows, lax.axis_index("lon") * cols]
     ).astype(f32)
     weights = (conv_weight, map_weight, map_bias, input_weight, hidden_weight, output_weight)
-    fg, conv_part, map_part, hid_part, small = run_main(
-        base, queries, latents, halo_of(latents), weights, dims
-    )
-    fg3 = fg.reshape(rows, cols, ch)
-    vmem = pl.BlockSpec(memory_space=pltpu.VMEM)
-    latent_grad = pl.pallas_call(
-        latent_kernel,
-        out_shape=jax.ShapeDtypeStruct((rows, cols, ch), f32),
-        in_specs=[vmem] * 6,
-        out_specs=vmem,
-        compiler_params=pltpu.CompilerParams(vmem_limit_bytes=32 << 20),
-        name="latent",
-    )(fg3, *halo_of(fg3), conv_weight)
-    conv_part, map_part, hid_part, small = lax.psum(
-        (conv_part, map_part, hid_part, small), ("lat", "lon")
-    )
+    fg, grads, small = run_main(base, queries, latents, halo_of(latents), weights, dims)
     scale = float(hits * group * dev_count) ** (-0.5)
     width = input_weight.shape[1]
-    small = small * scale
+    latent_grad, conv_grad, map_grad, hidden_grad, small = run_finish(
+        fg, conv_weight, grads, small, latents.shape, scale, width
+    )
     return (
         latent_grad,
-        conv_part.reshape(9, ch, ch) * scale,
-        map_part * scale,
+        conv_grad,
+        map_grad,
         small[0],
         jnp.stack([small[1, :width], small[1, width:], small[2, :width]]),
-        hid_part[None] * scale,
+        hidden_grad[None],
         small[2, width:],
     )
 

time: 268 us -> 149 us (0.56)
  waiting for transfers between devices: 80.3 us -> 3.36 us
  blocking collectives: 64.2 us -> 0 us
  Pallas kernels: 61.5 us -> 110 us
  between operations: 14.4 us -> 0.97 us
  starting transfers between devices: 32 us -> 21.5 us
  other arithmetic: 7.95 us -> 2.35 us
  local copies, waits for them, and re-layouts: 6.32 us -> 10.3 us
    psum x1 -> x0, waiting for transfers between devices: 77 us -> none  [on_device(): lax.psum((conv_part, map_part, hid_part, small), ('lat', 'lon'))]
    psum x1 -> x0, blocking collectives: 64.2 us -> none  [on_device(): lax.psum((conv_part, map_part, hid_part, small), ('lat', 'lon'))]
    pallas_call x1, Pallas kernels: 1.21 us -> 49.4 us  [run_finish(): pl.pallas_call(functools.partial(finish_kernel, (nx, ny, nz), scale), out...]
    mul x4 -> x0, other arithmetic: 5.57 us -> none  [the longest x1 3.42 us: on_device(): conv_part.reshape(9, ch, ch) * scale]
    ppermute x2 -> x1, starting transfers between devices: 8.31 us -> 3.51 us  [halo_of(): right = lax.ppermute(column(0), 'lon', west)]
    unnamed x22 -> x20, local copies, waits for them, and re-layouts: 0.06 us -> 4.09 us
    ppermute x2 -> x1, starting transfers between devices: 6.51 us -> 3.53 us  [halo_of(): top = lax.ppermute(tile[-1:], 'lat', up)]
    ppermute x2 -> x1, starting transfers between devices: 5.89 us -> 3.32 us  [halo_of(): bottom = lax.ppermute(tile[:1], 'lat', down)]
  transfers between devices with their start and end apart: 10 -> 5, of which waited for: 2 -> 1; matrix products, arithmetic and copies ran while one was open for 3% -> 5% of each run, Pallas kernels for 0% -> 0%
where the time goes in v2:
time: 149 us
  Pallas kernels  110 us (74%)
  starting transfers between devices  21.5 us (14%)
  local copies, waits for them, and re-layouts  10.3 us (7%)
  waiting for transfers between devices  3.36 us (2%)
  other arithmetic  2.35 us (2%)
    pallas_call x1, Pallas kernels, run_main(): pl.pallas_call(functools.partial(main_kernel, dims), out_shape=(jax.Shape...  60.2 us
    pallas_call x1, Pallas kernels, run_finish(): pl.pallas_call(functools.partial(finish_kernel, (nx, ny, nz), scale), out...  49.4 us
    all_to_all x1, starting transfers between devices, on_device(): lax.all_to_all(outgoing.reshape(dev_count, 1, 4 * group), ('lat', 'lon'),...  9.65 us
    unnamed x20, local copies, waits for them, and re-layouts  4.09 us
    ppermute x1, starting transfers between devices, halo_of(): top = lax.ppermute(tile[-1:], 'lat', up)  3.53 us
    ppermute x1, starting transfers between devices, halo_of(): right = lax.ppermute(column(0), 'lon', west)  3.51 us
    all_to_all x1, waiting for transfers between devices, on_device(): lax.all_to_all(outgoing.reshape(dev_count, 1, 4 * group), ('lat', 'lon'),...  3.35 us
    ppermute x1, starting transfers between devices, halo_of(): bottom = lax.ppermute(tile[:1], 'lat', down)  3.32 us
  transfers between devices with their start and end apart: 5, of which 1 were waited for; matrix products, arithmetic and copies ran while one was open for 5% of the time, Pallas kernels for 0%

profile of v2, /device:TPU:1, one launch (start us, length us, event | category | flops | bytes accessed | tf_op | source)
XLA Modules:
  0.0 149.0 jit_solution(2897190470969908600)
XLA Ops:
  0.7 0.9 fusion.10
  1.6 3.3 %collective-permute-start.1 = (bf16[1,16,256]{2,1,0:T(8,128)(2,1)S(1)}, bf16[1,16,256]{2,1,0:T(8,128)(2,1)S(1)}, u32[]{:S(2)}, u32[]{:S(2)}) collective-permute-start(bf16[1,16,256]{2,1,0:T(8,128)(2,1)S(1)} %get-tuple-element.28), channel_id=1, source_target_pairs={{16,0},{32,16},{48,32},{64,48},{80,64},{96,80},{112,96},{17,1},{33... | collective-permute-start | bytes 24584 | tf_op jit(solution)/shard_map/ppermute | solution.py:658
  4.9 3.5 %collective-permute-start = (bf16[1,16,256]{2,1,0:T(8,128)(2,1)S(1)}, bf16[1,16,256]{2,1,0:T(8,128)(2,1)S(1)}, u32[]{:S(2)}, u32[]{:S(2)}) collective-permute-start(bf16[1,16,256]{2,1,0:T(8,128)(2,1)S(1)} %get-tuple-element.29), channel_id=1, source_target_pairs={{0,16},{16,32},{32,48},{48,64},{64,80},{80,96},{96,112},{1,17},{17... | collective-permute-start | bytes 24584 | tf_op jit(solution)/shard_map/ppermute | solution.py:657
  8.4 0.8 reshape.124
  9.2 0.9 convert_element_type.17
  10.2 0.2 slice_reduce_fusion.2
  10.6 1.0 convolution_bitcast_fusion
  11.5 0.8 copy.31
  12.3 9.7 %all-to-all-start = ((f32[128,1,256]{2,1,0:T(1,128)}), f32[128,1,256]{2,1,0:T(1,128)S(1)}, u32[]{:S(2)}, u32[]{:S(2)}) async-start(f32[128,1,256]{2,1,0:T(1,128)} %copy.31), calls=%async_computation | async-start | bytes 262144 | tf_op jit(solution)/shard_map/all_to_all | solution.py:700
  22.0 0.9 fusion.9
  22.9 0.7 multiply_bitcast_fusion
  23.7 1.5 collective-permute-start.2
  25.2 3.5 %collective-permute-start.3 = (bf16[18,256]{1,0:T(8,128)(2,1)S(1)}, bf16[18,256]{1,0:T(8,128)(2,1)S(1)}, u32[]{:S(2)}, u32[]{:S(2)}) collective-permute-start(bf16[18,256]{1,0:T(8,128)(2,1)S(1)} %pad_maximum_fusion.1), channel_id=1, source_target_pairs={{1,0},{2,1},{3,2},{4,3},{5,4},{6,5},{7,6},{8,7},{9,8},{10,9},{11,1... | collective-permute-start | bytes 27656 | tf_op jit(solution)/shard_map/ppermute | solution.py:666
  28.7 3.3 %all-to-all-done = f32[128,1,256]{2,1,0:T(1,128)S(1)} async-done(((f32[128,1,256]{2,1,0:T(1,128)}), f32[128,1,256]{2,1,0:T(1,128)S(1)}, u32[]{:S(2)}, u32[]{:S(2)}) %all-to-all-start) | async-done | bytes 131104 | tf_op jit(solution)/shard_map/all_to_all | solution.py:700
  33.1 0.3 stack.31.q_ref
  33.6 60.2 %queries.1 = (bf16[256,256]{1,0:T(8,128)(2,1)S(1)}, f32[17,256,256]{2,1,0:T(8,128)}, f32[8,1024]{1,0:T(8,128)S(1)}) custom-call(f32[2]{0:T(128)S(1)} %add_convert_fusion.base_ref, f32[8,8192]{1,0:T(8,128)S(1)} %stack.31.q_ref, bf16[16,16,256]{2,1,0:T(8,128)(2,1)S(1)} %copy-done.3, bf16[16,256]{1,0:T(8,128)(2,1)S(1)} %bitcast.42, ...), custom_call_target="tpu_custom_call" | custom-call | tf_op jit(solution)/shard_map/queries/pallas_call | solution.py:262
  93.8 49.4 %finish.1 = (f32[16,16,256]{2,1,0:T(8,128)S(1)}, f32[9,256,256]{2,1,0:T(8,128)S(1)}, f32[256,1024]{1,0:T(8,128)S(1)}, f32[512,512]{1,0:T(8,128)S(1)}, f32[8,1024]{1,0:T(8,128)S(1)}) custom-call(bf16[256,256]{1,0:T(8,128)(2,1)S(1)} %get-tuple-element.15.fg_ref, bf16[9,256,256]{2,1,0:T(8,128)(2,1)S(1)} %copy-done, f32[17,256,256]{2,1,0:T(8,128)} %get-tuple-element.16.wg_ref, ...), custom_call_target="tpu_custom_call" | custom-call | tf_op jit(solution)/shard_map/finish/pallas_call | solution.py:607
  143.2 0.6 slice.78
  143.8 0.6 fusion.12
  144.4 0.6 pad_maximum_fusion.2
  145.0 0.7 copy.49
  145.7 1.4 copy.50
  147.1 1.0 copy.51
  148.0 1.0 copy.52
  (41 shorter events, 1.4 us)
Async XLA Ops:
  0.6 32.9 %copy-start.3 = (bf16[16,16,256]{2,1,0:T(8,128)(2,1)S(1)}, bf16[16,16,256]{2,1,0:T(8,128)(2,1)}, u32[]{:S(2)}) copy-start(bf16[16,16,256]{2,1,0:T(8,128)(2,1)} %center_ref.1) | copy-start | bytes 393220
  0.6 32.9 %copy-start = (bf16[9,256,256]{2,1,0:T(8,128)(2,1)S(1)}, bf16[9,256,256]{2,1,0:T(8,128)(2,1)}, u32[]{:S(2)}) copy-start(bf16[9,256,256]{2,1,0:T(8,128)(2,1)} %convw_ref.1) | copy-start | bytes 3538948
  0.7 32.9 %copy-start.6 = (f32[512]{0:T(512)S(1)}, f32[512]{0:T(512)}, u32[]{:S(2)}) copy-start(f32[512]{0:T(512)} %param.17) | copy-start | bytes 6148
  0.7 32.9 %copy-start.2 = (bf16[1,512,512]{2,1,0:T(8,128)(2,1)S(1)}, bf16[1,512,512]{2,1,0:T(8,128)(2,1)}, u32[]{:S(2)}) copy-start(bf16[1,512,512]{2,1,0:T(8,128)(2,1)} %param.16) | copy-start | bytes 1572868
  0.7 32.9 %copy-start.4 = (f32[3,512]{1,0:T(4,128)S(1)}, f32[3,512]{1,0:T(4,128)}, u32[]{:S(2)}) copy-start(f32[3,512]{1,0:T(4,128)} %inw_ref.1) | copy-start | bytes 18436
  0.7 32.9 %copy-start.5 = (f32[1024]{0:T(1024)S(1)}, f32[1024]{0:T(1024)}, u32[]{:S(2)}) copy-start(f32[1024]{0:T(1024)} %param.14) | copy-start | bytes 12292
  0.7 32.9 %copy-start.1 = (bf16[256,1024]{1,0:T(8,128)(2,1)S(1)}, bf16[256,1024]{1,0:T(8,128)(2,1)}, u32[]{:S(2)}) copy-start(bf16[256,1024]{1,0:T(8,128)(2,1)} %mapw_ref.1) | copy-start | bytes 1572868
  1.6 22.1 %collective-permute-start.1 = (bf16[1,16,256]{2,1,0:T(8,128)(2,1)S(1)}, bf16[1,16,256]{2,1,0:T(8,128)(2,1)S(1)}, u32[]{:S(2)}, u32[]{:S(2)}) collective-permute-start(bf16[1,16,256]{2,1,0:T(8,128)(2,1)S(1)} %get-tuple-element.28), channel_id=1, source_target_pairs={{16,0},{32,16},{48,32},{64,48},{80,64},{96,80},{112,96},{17,1},{33... | collective-permute-start | bytes 24584 | tf_op jit(solution)/shard_map/ppermute | solution.py:658
  4.9 18.8 %collective-permute-start = (bf16[1,16,256]{2,1,0:T(8,128)(2,1)S(1)}, bf16[1,16,256]{2,1,0:T(8,128)(2,1)S(1)}, u32[]{:S(2)}, u32[]{:S(2)}) collective-permute-start(bf16[1,16,256]{2,1,0:T(8,128)(2,1)S(1)} %get-tuple-element.29), channel_id=1, source_target_pairs={{0,16},{16,32},{32,48},{48,64},{64,80},{80,96},{96,112},{1,17},{17... | collective-permute-start | bytes 24584 | tf_op jit(solution)/shard_map/ppermute | solution.py:657
  12.3 19.7 %all-to-all-start = ((f32[128,1,256]{2,1,0:T(1,128)}), f32[128,1,256]{2,1,0:T(1,128)S(1)}, u32[]{:S(2)}, u32[]{:S(2)}) async-start(f32[128,1,256]{2,1,0:T(1,128)} %copy.31), calls=%async_computation | async-start | bytes 262144 | tf_op jit(solution)/shard_map/all_to_all | solution.py:700
  23.7 9.7 %collective-permute-start.2 = (bf16[18,256]{1,0:T(8,128)(2,1)S(1)}, bf16[18,256]{1,0:T(8,128)(2,1)S(1)}, u32[]{:S(2)}, u32[]{:S(2)}) collective-permute-start(bf16[18,256]{1,0:T(8,128)(2,1)S(1)} %pad_maximum_fusion), channel_id=1, source_target_pairs={{0,1},{1,2},{2,3},{3,4},{4,5},{5,6},{6,7},{7,8},{8,9},{9,10},{10,1... | collective-permute-start | bytes 27656 | tf_op jit(solution)/shard_map/ppermute | solution.py:665
  25.2 8.3 %collective-permute-start.3 = (bf16[18,256]{1,0:T(8,128)(2,1)S(1)}, bf16[18,256]{1,0:T(8,128)(2,1)S(1)}, u32[]{:S(2)}, u32[]{:S(2)}) collective-permute-start(bf16[18,256]{1,0:T(8,128)(2,1)S(1)} %pad_maximum_fusion.1), channel_id=1, source_target_pairs={{1,0},{2,1},{3,2},{4,3},{5,4},{6,5},{7,6},{8,7},{9,8},{10,9},{11,1... | collective-permute-start | bytes 27656 | tf_op jit(solution)/shard_map/ppermute | solution.py:666

commit v3 on v2

v3 whole, which is shorter than its diff:
```python
import functools
import math

import jax
import jax.numpy as jnp
import numpy as np
from jax import lax
from jax.experimental import pallas as pl
from jax.experimental.pallas import tpu as pltpu
from jax.sharding import PartitionSpec as P

BLOCK = 128
LEVELS = 37
SUB = 6
OMEGA = 30.0
INV_TURN = float(1.0 / (2.0 * math.pi))
TURN = float(2.0 * math.pi)
TILE = 512
ROWS = 32
MCH = 512
NCH = 256
GM = 272
SPLIT = 10
CHUNKS = ((0, 6), (6, 12), (12, 17))


def _fit():
    nodes = np.cos((2 * np.arange(400) + 1) * np.pi / 800)
    r = (nodes + 1) / 4
    z = r * r
    sine = np.sqrt(2.0) * np.sin(np.pi * r)
    cosine = np.sqrt(2.0) * np.cos(np.pi * r)
    sa = np.stack([r * z**k for k in range(4)], 1)
    ca = np.stack([z**k for k in range(5)], 1)
    return (
        [float(v) for v in np.linalg.lstsq(sa, sine, rcond=None)[0]],
        [float(v) for v in np.linalg.lstsq(ca, cosine, rcond=None)[0]],
    )


SIN_C, COS_C = _fit()


def sincos_turns(t):
    r = t - jnp.round(t)
    z = r * r
    s = r * (SIN_C[0] + z * (SIN_C[1] + z * (SIN_C[2] + z * SIN_C[3])))
    c = COS_C[0] + z * (COS_C[1] + z * (COS_C[2] + z * (COS_C[3] + z * COS_C[4])))
    return s * c, 1.0 - s * s


def dot(a, b):
    return jnp.dot(a, b, preferred_element_type=jnp.float32)


def dot_nt(a, b):
    return lax.dot_general(a, b, (((1,), (1,)), ((), ())), preferred_element_type=jnp.float32)


def dot_tn(a, b):
    return lax.dot_general(a, b, (((0,), (0,)), ((), ())), preferred_element_type=jnp.float32)


def split2(v):
    hi = v.astype(jnp.bfloat16)
    return hi, (v - hi.astype(jnp.float32)).astype(jnp.bfloat16)


def split3(v):
    hi = v.astype(jnp.bfloat16).astype(jnp.float32)
    mid = (v - hi).astype(jnp.bfloat16).astype(jnp.float32)
    return hi, mid, v - hi - mid


def shifted(center, top, bottom, left, right):
    rows, cols, ch = center.shape
    total = (rows + 2) * cols
    mid = jnp.concatenate([top, center.reshape(rows * cols, ch), bottom], axis=0)
    mid32 = mid.astype(jnp.float32)
    col = lax.broadcasted_iota(jnp.int32, (rows + 2, cols, ch), 1)
    low = pltpu.roll(mid32, 1, 0).reshape(rows + 2, cols, ch)
    high = pltpu.roll(mid32, total - 1, 0).reshape(rows + 2, cols, ch)
    low = jnp.where(col == 0, left.astype(jnp.float32)[:, None, :], low)
    high = jnp.where(col == cols - 1, right.astype(jnp.float32)[:, None, :], high)
    return (
        low.reshape(total, ch).astype(jnp.bfloat16),
        mid,
        high.reshape(total, ch).astype(jnp.bfloat16),
    )


def main_kernel(
    dims,
    base_ref,
    q_ref,
    center_ref,
    top_ref,
    bottom_ref,
    left_ref,
    right_ref,
    convw_ref,
    mapw_ref,
    mapb_ref,
    inw_ref,
    hid_ref,
    outw_ref,
    fg_ref,
    grads_ref,
    small_ref,
    hidg_ref,
    x3_ref,
    feat_ref,
    tab0_ref,
    tab1_ref,
    wcol_ref,
    g_ref,
    og_ref,
    *pairs,
):
    lat_cells, lon_cells = dims
    rows, cols, ch = center_ref.shape
    cells = rows * cols
    width = inw_ref.shape[1]
    rhs_refs, c0_refs, d_refs = pairs[0:4], pairs[4:8], pairs[8:12]
    ta_ref, tc_ref, te_ref = pairs[12:]
    tile = rhs_refs[0].shape[1]
    tiles = q_ref.shape[1] // tile
    f32 = jnp.float32
    bf16 = jnp.bfloat16

    x3 = shifted(center_ref[...], top_ref[...], bottom_ref[...], left_ref[...], right_ref[...])
    for b in range(3):
        x3_ref[:, b * ch : (b + 1) * ch] = x3[b]
    acc = dot(x3_ref[0:cells, :], convw_ref[0])
    for a in (1, 2):
        acc += dot(x3_ref[a * cols : a * cols + cells, :], convw_ref[a])
    feat_ref[...] = acc.astype(bf16)

    shift = dot(feat_ref[...], mapw_ref[...]) + mapb_ref[...]
    cell = lax.broadcasted_iota(jnp.int32, (cells, width), 0)
    row_f = (cell // cols).astype(f32)
    col_f = (cell % cols).astype(f32)
    lat_c = ((base_ref[0] + row_f) * SUB + 0.5) * (2.0 / (lat_cells * SUB)) - 1.0
    lon_c = ((base_ref[1] + col_f) * SUB + 0.5) * (2.0 / (lon_cells * SUB)) - 1.0
    lev_c = 1.0 / LEVELS - 1.0
    linear = (
        lat_c * inw_ref[0:1, :] + lon_c * inw_ref[1:2, :] + lev_c * inw_ref[2:3, :]
    )
    turn0 = (OMEGA * linear + shift[:, :width]) * INV_TURN
    turn0 = turn0 - jnp.round(turn0)
    hi, lo = split2(turn0.T)
    tab0_ref[:, 0:cells] = hi
    tab0_ref[:, cells : 2 * cells] = lo
    turn1 = shift[:, width:] * INV_TURN
    turn1 = (turn1 - jnp.round(turn1)) * TURN
    hi, lo = split2(turn1.T)
    tab1_ref[:, width : width + cells] = hi
    tab1_ref[:, width + cells : width + 2 * cells] = lo
    tab1_ref[:, 0:width] = hid_ref[...].astype(f32).T.astype(bf16)
    steps = (
        2.0 * OMEGA * INV_TURN / (lat_cells * SUB),
        2.0 * OMEGA * INV_TURN / (lon_cells * SUB),
        2.0 * OMEGA * INV_TURN / LEVELS,
    )
    parts = [split3(inw_ref[c : c + 1, :] * steps[c]) for c in range(3)]
    ext_row = lax.broadcasted_iota(jnp.int32, (128, width), 0)
    ext = jnp.zeros((128, width), f32)
    for level in range(3):
        for c in range(3):
            ext = jnp.where(ext_row == level * 3 + c, parts[c][level], ext)
    tab0_ref[:, 2 * cells : 2 * cells + 128] = ext.T.astype(bf16)
    wcol_ref[...] = jnp.broadcast_to(outw_ref[...], (128, width)).T

    oh0 = width
    oh1 = width + cells
    ex0 = width + 2 * cells
    for rhs_ref in rhs_refs:
        rhs_ref[ex0:, :] = jnp.zeros((128, tile), bf16)
    g_ref[...] = jnp.zeros_like(g_ref)
    hidg_ref[...] = jnp.zeros_like(hidg_ref)
    og_ref[...] = jnp.zeros_like(og_ref)

    def encode(k, at):
        k = k % 4
        rhs_ref = rhs_refs[k]
        cell_q = q_ref[0:1, at]
        for m in range(0, cells, 64):
            iota = (lax.broadcasted_iota(jnp.int32, (64, tile), 0) + m).astype(f32)
            onehot = jnp.where(iota == cell_q, 1.0, 0.0).astype(bf16)
            rhs_ref[oh0 + m : oh0 + m + 64, :] = onehot
            rhs_ref[oh1 + m : oh1 + m + 64, :] = onehot
        r = lax.broadcasted_iota(jnp.int32, (16, tile), 0)
        ints = jnp.where(
            r % 3 == 0, q_ref[1:2, at], jnp.where(r % 3 == 1, q_ref[2:3, at], q_ref[3:4, at])
        )
        rhs_ref[ex0 : ex0 + 16, :] = jnp.where(r < 9, ints, 0.0).astype(bf16)

    def dots(out_ref, a_ref, b_ref, b_rows):
        def piece(m, n):
            def run():
                out_ref[m : m + MCH, n : n + NCH] = dot(
                    a_ref[m : m + MCH, :], b_ref[b_rows, n : n + NCH]
                )

            return run

        return [piece(m, n) for n in range(0, tile, NCH) for m in range(0, width, MCH)]

    def first_dot(k):
        k = k % 4

        return dots(ta_ref, tab0_ref, rhs_refs[k], slice(oh0, ex0 + 128))

    def second_dot(k):
        k = k % 4

        return dots(tc_ref, tab1_ref, rhs_refs[k], slice(0, ex0))

    def back_dot(k):
        k = k % 4

        return dots(te_ref, hid_ref, d_refs[k], slice(width, 2 * width))

    def first_sine(k):
        k = k % 4

        def piece(m):
            def run():
                s, c = sincos_turns(ta_ref[m : m + ROWS, :])
                rhs_refs[k][m : m + ROWS, :] = s.astype(bf16)
                c0_refs[k][m : m + ROWS, :] = c

            return run

        return [piece(m) for m in range(0, width, ROWS)]

    def second_sine(k, at):
        k = k % 4

        def piece(m):
            def run():
                cot = q_ref[4:5, at]
                s, c = sincos_turns(tc_ref[m : m + ROWS, :] * INV_TURN)
                sw = s * cot
                cc = c * cot
                w = wcol_ref[m : m + ROWS, :]
                og = og_ref[m : m + ROWS, :]
                for n in range(0, tile, 128):
                    og = og + sw[:, n : n + 128]
                    d_refs[k][width + m : width + m + ROWS, n : n + 128] = (
                        cc[:, n : n + 128] * w
                    ).astype(bf16)
                og_ref[m : m + ROWS, :] = og

            return run

        return [piece(m) for m in range(0, width, ROWS)]

    def back_cosine(k):
        k = k % 4

        def piece(m):
            def run():
                d_refs[k][m : m + ROWS, :] = (
                    te_ref[m : m + ROWS, :] * c0_refs[k][m : m + ROWS, :]
                ).astype(bf16)

            return run

        return [piece(m) for m in range(0, width, ROWS)]

    def hidden_sum(k):
        k = k % 4

        def piece(m, n):
            def run():
                hidg_ref[m : m + MCH, n : n + NCH] += dot_nt(
                    rhs_refs[k][m : m + MCH, :], d_refs[k][width + n : width + n + NCH, :]
                )

            return run

        return [piece(m, n) for n in range(0, width, NCH) for m in range(0, width, MCH)]

    def cell_sum(k):
        k = k % 4

        def piece(m, n):
            def run():
                e = min(m + GM, cells + 16)
                g_ref[m:e, n : n + NCH] += dot_nt(
                    rhs_refs[k][oh1 + m : oh1 + e, :], d_refs[k][n : n + NCH, :]
                )

            return run

        return [piece(m, n) for n in range(0, 2 * width, NCH) for m in range(0, cells + 16, GM)]

    def weave(first, second):
        i = j = 0
        while i < len(first) or j < len(second):
            if j >= len(second) or (i < len(first) and i * len(second) <= j * len(first)):
                first[i]()
                i += 1
            else:
                second[j]()
                j += 1

    def at_tile(i):
        return pl.ds(pl.multiple_of(i * tile, tile), tile)

    def stage(u, i, count):
        weave(
            back_dot(u) + (second_dot(u + 1) if count > 1 else []),
            first_sine(u + 2) if count > 2 else [],
        )
        ahead = []
        if count > 3:
            encode(u + 3, at_tile(i + 3))
            ahead = first_dot(u + 3)
        late = second_sine(u + 1, at_tile(i + 1)) if count > 1 else []
        weave(ahead + hidden_sum(u), back_cosine(u) + late[: len(late) * SPLIT // 16])
        weave(cell_sum(u), late[len(late) * SPLIT // 16 :])

    for i in range(3):
        encode(i, at_tile(i))
    weave(first_dot(0), [])
    weave([], first_sine(0))
    weave(first_dot(1) + second_dot(0), [])
    weave([], first_sine(1))
    weave(first_dot(2), second_sine(0, at_tile(0)))

    def step(i, carry):
        for u in range(4):
            stage(u, 4 * i + u, 4)
        return carry

    lax.fori_loop(0, tiles // 4 - 1, step, 0)
    for u in range(4):
        stage(u, tiles - 4 + u, 4 - u)

    g = g_ref[0:cells, :]
    hi, lo = split2(g)
    fg = (dot_nt(hi, mapw_ref[...]) + dot_nt(lo, mapw_ref[...])).astype(bf16)
    fg_ref[...] = fg
    feat_t = feat_ref[...].astype(f32).T.astype(bf16)
    grad = dot(feat_t, hi) + dot(feat_t, lo)
    for k in range(4):
        grads_ref[9 + k] = grad[:, k * ch : (k + 1) * ch]
        r, c = k // 2 * ch, k % 2 * ch
        grads_ref[13 + k] = hidg_ref[r : r + ch, c : c + ch]
    for a in range(3):
        grad = dot_tn(x3_ref[a * cols : a * cols + cells, :], fg)
        for b in range(3):
            grads_ref[3 * a + b] = grad[b * ch : (b + 1) * ch, :]
    bias = jnp.sum(g, axis=0, keepdims=True)
    g0 = g[:, :width]
    ig0 = jnp.sum(lat_c * g0, axis=0, keepdims=True) + (2.0 / (lat_cells * SUB)) * g_ref[
        cells : cells + 1, :width
    ]
    ig1 = jnp.sum(lon_c * g0, axis=0, keepdims=True) + (2.0 / (lon_cells * SUB)) * g_ref[
        cells + 1 : cells + 2, :width
    ]
    ig2 = lev_c * bias[:, :width] + (2.0 / LEVELS) * g_ref[cells + 2 : cells + 3, :width]
    og = jnp.sum(og_ref[...].T, axis=0, keepdims=True)
    small_ref[...] = jnp.zeros_like(small_ref)
    small_ref[0:1, :] = bias
    small_ref[1:2, 0:width] = OMEGA * ig0
    small_ref[1:2, width:] = OMEGA * ig1
    small_ref[2:3, 0:width] = OMEGA * ig2
    small_ref[2:3, width:] = og


def run_main(base, queries, center, halo, weights, dims):
    conv_weight, map_weight, map_bias, input_weight, hidden_weight, output_weight = weights
    rows, cols, ch = center.shape
    cells = rows * cols
    width = input_weight.shape[1]
    f32 = jnp.float32
    bf16 = jnp.bfloat16
    vmem = pl.BlockSpec(memory_space=pltpu.VMEM)
    return pl.pallas_call(
        functools.partial(main_kernel, dims),
        out_shape=(
            jax.ShapeDtypeStruct((cells, ch), bf16),
            jax.ShapeDtypeStruct((17, ch, ch), f32),
            jax.ShapeDtypeStruct((8, 2 * width), f32),
        ),
        in_specs=[pl.BlockSpec(memory_space=pltpu.SMEM)] + [vmem] * 12,
        out_specs=(vmem,) * 3,
        scratch_shapes=[
            pltpu.VMEM((width, width), f32),
            pltpu.VMEM(((rows + 2) * cols, 3 * ch), bf16),
            pltpu.VMEM((cells, ch), bf16),
            pltpu.VMEM((width, 2 * cells + 128), bf16),
            pltpu.VMEM((width, width + 2 * cells), bf16),
            pltpu.VMEM((width, 128), f32),
            pltpu.VMEM((cells + 16, 2 * width), f32),
            pltpu.VMEM((width, 128), f32),
        ]
        + [pltpu.VMEM((width + 2 * cells + 128, TILE), bf16)] * 4
        + [pltpu.VMEM((width, TILE), f32)] * 4
        + [pltpu.VMEM((2 * width, TILE), bf16)] * 4
        + [pltpu.VMEM((width, TILE), f32)] * 3,
        compiler_params=pltpu.CompilerParams(vmem_limit_bytes=48 << 20),
        name="queries",
    )(
        base,
        queries,
        center,
        *halo,
        conv_weight.reshape(3, 3 * ch, ch),
        map_weight,
        map_bias.reshape(1, -1),
        input_weight,
        hidden_weight[0],
        output_weight.reshape(1, -1),
    )


AROUND = ((-1, 0), (1, 0), (0, -1), (0, 1), (-1, -1), (-1, 1), (1, -1), (1, 1))


def remote(src, dst, send, recv, device):
    return pltpu.make_async_remote_copy(
        src_ref=src,
        dst_ref=dst,
        send_sem=send,
        recv_sem=recv,
        device_id=device,
        device_id_type=pl.DeviceIdType.MESH,
    )


def at_rim(da, db):
    lat_n = lax.axis_size("lat")
    lon_n = lax.axis_size("lon")
    lat = lax.rem(lax.axis_index("lat") + da + lat_n, lat_n)
    return (lat, lax.rem(lax.axis_index("lon") + db + lon_n, lon_n))


def meet(peers):
    barrier = pltpu.get_barrier_semaphore()
    for peer in peers:
        pl.semaphore_signal(barrier, inc=1, device_id=peer, device_id_type=pl.DeviceIdType.MESH)

    def wait():
        pl.semaphore_wait(barrier, len(peers))

    return wait


def rim_copies(flat_ref, cols, col_s, row_r, col_r, send, recv):
    cells = flat_ref.shape[0]
    first = flat_ref.at[pl.ds(0, cols)]
    last = flat_ref.at[pl.ds(cells - cols, cols)]
    return [
        remote(last, row_r.at[0], send.at[0], recv.at[0], at_rim(1, 0)),
        remote(first, row_r.at[1], send.at[1], recv.at[1], at_rim(-1, 0)),
        remote(col_s.at[0], col_r.at[0], send.at[2], recv.at[2], at_rim(0, 1)),
        remote(col_s.at[1], col_r.at[1], send.at[3], recv.at[3], at_rim(0, -1)),
        remote(last, row_r.at[2], send.at[4], recv.at[4], at_rim(1, 1)),
        remote(last, row_r.at[3], send.at[5], recv.at[5], at_rim(1, -1)),
        remote(first, row_r.at[4], send.at[6], recv.at[6], at_rim(-1, 1)),
        remote(first, row_r.at[5], send.at[7], recv.at[7], at_rim(-1, -1)),
    ]


def edge_columns(flat, rows, cols, col_s):
    tile = flat.astype(jnp.float32).reshape(rows, cols, flat.shape[1])
    col_s[0] = tile[:, cols - 1, :].astype(flat.dtype)
    col_s[1] = tile[:, 0, :].astype(flat.dtype)


def rim_values(cols, row_r, col_r):
    f32 = jnp.float32
    bf16 = jnp.bfloat16
    lat = lax.axis_index("lat")
    up = jnp.where(lat > 0, 1.0, 0.0).astype(f32)
    down = jnp.where(lat < lax.axis_size("lat") - 1, 1.0, 0.0).astype(f32)
    top = (row_r[0].astype(f32) * up).astype(bf16)
    bottom = (row_r[1].astype(f32) * down).astype(bf16)
    nw = row_r[2].astype(f32)[cols - 1 : cols] * up
    ne = row_r[3].astype(f32)[0:1] * up
    sw = row_r[4].astype(f32)[cols - 1 : cols] * down
    se = row_r[5].astype(f32)[0:1] * down
    left = jnp.concatenate([nw, col_r[0].astype(f32), sw], axis=0)
    right = jnp.concatenate([ne, col_r[1].astype(f32), se], axis=0)
    return top, bottom, left.astype(bf16), right.astype(bf16)


def front_kernel(
    data_ref,
    owner_ref,
    tile_ref,
    out_ref,
    top_ref,
    bottom_ref,
    left_ref,
    right_ref,
    go,
    mid,
    turned,
    row_r,
    col_s,
    col_r,
    send,
    recv,
    hsem_s,
    hsem_r,
):
    lat = lax.axis_index("lat")
    lon = lax.axis_index("lon")
    lat_n, lon_n, words = out_ref.shape
    hits = data_ref.shape[0]
    cols = top_ref.shape[0]
    rows = tile_ref.shape[0] // cols

    def at_lon(d):
        return (lat, lax.rem(lon + d, lon_n))

    def at_lat(d):
        return (lax.rem(lat + d, lat_n), lon)

    peers = [at_lon(d) for d in range(1, lon_n)] + [at_lat(d) for d in range(1, lat_n)]
    wait = meet(peers + [at_rim(da, db) for da, db in AROUND])

    at = lax.broadcasted_iota(jnp.int32, (lat_n * lon_n, hits), 0)
    device = lax.rem(at, lat_n) * lon_n + lax.div(at, lat_n)
    pick = jnp.where(device == owner_ref[...], 1.0, 0.0).astype(jnp.float32)
    picked = jnp.dot(
        pick, data_ref[...], precision=lax.Precision.HIGHEST, preferred_element_type=jnp.float32
    )
    go[...] = picked.reshape(lon_n, lat_n, words)
    mid[lon] = go[lon]
    edge_columns(tile_ref[...], rows, cols, col_s)
    wait()
    one = []
    for d in range(1, lon_n):
        peer = lax.rem(lon + d, lon_n)
        one.append(remote(go.at[peer], mid.at[lon], send.at[d], recv.at[d], at_lon(d)))
        one[-1].start()
    rim = rim_copies(tile_ref, cols, col_s, row_r, col_r, hsem_s, hsem_r)
    for item in rim:
        item.start()
    for item in one:
        item.wait()
    for k in range(lat_n):
        turned[k] = mid[:, k, :]
    out_ref[lat] = turned[lat]
    two = []
    for d in range(1, lat_n):
        peer = lax.rem(lat + d, lat_n)
        two.append(
            remote(
                turned.at[peer],
                out_ref.at[lat],
                send.at[lon_n + d],
                recv.at[lon_n + d],
                at_lat(d),
            )
        )
        two[-1].start()
    for item in rim:
        item.wait()
    top, bottom, left, right = rim_values(cols, row_r, col_r)
    top_ref[...] = top
    bottom_ref[...] = bottom
    left_ref[...] = left
    right_ref[...] = right
    for item in two:
        item.wait()


def run_front(data, owner, tile, lat_n, lon_n):
    rows, cols, ch = tile.shape
    hits, words = data.shape
    f32 = jnp.float32
    bf16 = jnp.bfloat16
    dma = pltpu.SemaphoreType.DMA
    vmem = pl.BlockSpec(memory_space=pltpu.VMEM)
    return pl.pallas_call(
        front_kernel,
        out_shape=(
            jax.ShapeDtypeStruct((lat_n, lon_n, words), f32),
            jax.ShapeDtypeStruct((cols, ch), bf16),
            jax.ShapeDtypeStruct((cols, ch), bf16),
            jax.ShapeDtypeStruct((rows + 2, ch), bf16),
            jax.ShapeDtypeStruct((rows + 2, ch), bf16),
        ),
        in_specs=[vmem] * 3,
        out_specs=(vmem,) * 5,
        scratch_shapes=[
            pltpu.VMEM((lon_n, lat_n, words), f32),
            pltpu.VMEM((lon_n, lat_n, words), f32),
            pltpu.VMEM((lat_n, lon_n, words), f32),
            pltpu.VMEM((6, cols, ch), bf16),
            pltpu.VMEM((2, rows, ch), bf16),
            pltpu.VMEM((2, rows, ch), bf16),
            dma((lon_n + lat_n,)),
            dma((lon_n + lat_n,)),
            dma((8,)),
            dma((8,)),
        ],
        compiler_params=pltpu.CompilerParams(
            vmem_limit_bytes=16 << 20, collective_id=2, has_side_effects=True
        ),
        name="front",
    )(data, owner.reshape(1, hits), tile.reshape(rows * cols, ch))


def finish_kernel(
    sizes,
    chunks,
    scale,
    fg_ref,
    convw_ref,
    wg_ref,
    small_ref,
    latent_ref,
    half,
    other,
    total_ref,
    send1,
    recv1,
    acc1,
    send2,
    recv2,
    acc2,
    send3,
    recv3,
    slots4,
    pair_s,
    x_s,
    y_s,
    z_s,
    row_r,
    col_s,
    col_r,
    sem_s,
    sem_r,
    ssem_s,
    ssem_r,
    hsem_s,
    hsem_r,
):
    nx, ny, nz = sizes
    bf16 = jnp.bfloat16
    f32 = jnp.float32
    lat = lax.axis_index("lat")
    lon = lax.axis_index("lon")
    z, c = lax.div(lat, 2), lax.rem(lat, 2)
    x, y = lax.div(lon, ny), lax.rem(lon, ny)
    blocks, rows, lanes = half.shape
    quarter = rows // nx
    final = quarter // ny

    def at_pair():
        return (lat + 1 - 2 * c, lon)

    def at_x(d):
        return (lat, lax.rem(x + d, nx) * ny + y)

    def at_y(d):
        return (lat, x * ny + lax.rem(y + d, ny))

    def at_z(d):
        return (lax.rem(z + d, nz) * 2 + c, lon)

    def at_first(d):
        return (lat, (1 - c) * at_x(d)[1] + c * at_y(d)[1])

    def at_second(d):
        return (lat, c * at_x(d)[1] + (1 - c) * at_y(d)[1])

    first = (1 - c) * x + c * y
    second = c * x + (1 - c) * y

    peers = [at_pair()]
    peers += [at_x(d) for d in range(1, nx)]
    peers += [at_y(d) for d in range(1, ny)]
    peers += [at_z(d) for d in range(1, nz)]
    peers += [at_rim(da, db) for da, db in AROUND]
    wait = meet(peers)

    tile_rows, cols, ch = latent_ref.shape
    cells = tile_rows * cols
    keep = pl.ds(pl.multiple_of(c * lanes, lanes), lanes)
    give = pl.ds(pl.multiple_of((1 - c) * lanes, lanes), lanes)
    mine = pl.ds(pl.multiple_of(first * quarter, quarter), quarter)
    ours = pl.ds(pl.multiple_of(second * final, final), final)
    place = pl.ds(pl.multiple_of(first * quarter + second * final, final), final)

    def each(chunk, body):
        def one(b, carry):
            body(b)
            return carry

        lax.fori_loop(chunk[0], chunk[1], one, 0)

    def to_send1(b):
        send1[b] = wg_ref[b, :, give].astype(bf16)

    edge_columns(fg_ref[...], tile_rows, cols, col_s)
    pair_s[c] = small_ref[...]
    each(chunks[0], to_send1)
    wait()
    rim = rim_copies(fg_ref, cols, col_s, row_r, col_r, hsem_s, hsem_r)
    for item in rim:
        item.start()
    q1 = remote(pair_s.at[c], pair_s.at[c], ssem_s.at[0], ssem_r.at[0], at_pair())
    q1.start()

    def part(k):
        return pl.ds(chunks[k][0], chunks[k][1] - chunks[k][0])

    p1 = []
    for k in range(len(chunks)):
        if k > 0:
            each(chunks[k], to_send1)
        p1.append(
            remote(
                send1.at[part(k)], recv1.at[part(k)], sem_s.at[k, 0], sem_r.at[k, 0], at_pair()
            )
        )
        p1[-1].start()

    q1.wait()
    x_s[x] = pair_s[0] + pair_s[1]
    q2 = [remote(x_s.at[x], x_s.at[x], ssem_s.at[d], ssem_r.at[d], at_x(d)) for d in range(1, nx)]
    for item in q2:
        item.start()

    def add1(b):
        v = wg_ref[b, :, keep] + recv1[b].astype(f32)
        acc1[b] = v
        send2[b] = v.astype(bf16)

    p2 = []
    for k in range(len(chunks)):
        p1[k].wait()
        each(chunks[k], add1)
        group = []
        for d in range(1, nx):
            target = lax.rem(first + d, nx)
            group.append(
                remote(
                    send2.at[part(k), pl.ds(pl.multiple_of(target * quarter, quarter), quarter), :],
                    recv2.at[d - 1, part(k)],
                    sem_s.at[k, d],
                    sem_r.at[k, d],
                    at_first(d),
                )
            )
            group[-1].start()
        p2.append(group)

    for item in q2:
        item.wait()
    y_s[y] = (x_s[0] + x_s[1]) + (x_s[2] + x_s[3])
    q3 = [
        remote(y_s.at[y], y_s.at[y], ssem_s.at[3 + d], ssem_r.at[3 + d], at_y(d))
        for d in range(1, ny)
    ]
    for item in q3:
        item.start()

    for item in rim:
        item.wait()
    top, bottom, left, right = rim_values(cols, row_r, col_r)
    x3 = shifted(fg_ref[...].reshape(tile_rows, cols, ch), top, bottom, left, right)
    acc = None
    for a in (-1, 0, 1):
        start = (1 - a) * cols
        for b in (-1, 0, 1):
            piece = dot_nt(x3[1 - b][start : start + cells], convw_ref[3 * (a + 1) + b + 1])
            acc = piece if acc is None else acc + piece
    latent_ref[...] = acc.reshape(tile_rows, cols, ch)

    def add2(b):
        v = acc1[b, mine, :]
        for d in range(nx - 1):
            v += recv2[d, b].astype(f32)
        acc2[b] = v
        send3[b] = v.astype(bf16)

    p3 = []
    for k in range(len(chunks)):
        for item in p2[k]:
            item.wait()
        each(chunks[k], add2)
        group = []
        for d in range(1, ny):
            target = lax.rem(second + d, ny)
            group.append(
                remote(
                    send3.at[part(k), pl.ds(pl.multiple_of(target * final, final), final), :],
                    recv3.at[d - 1, part(k)],
                    sem_s.at[k, 3 + d],
                    sem_r.at[k, 3 + d],
                    at_second(d),
                )
            )
            group[-1].start()
        p3.append(group)

    for item in q3:
        item.wait()
    z_s[z] = (y_s[0] + y_s[1]) + (y_s[2] + y_s[3])
    q4 = [
        remote(z_s.at[z], z_s.at[z], ssem_s.at[6 + d], ssem_r.at[6 + d], at_z(d))
        for d in range(1, nz)
    ]
    for item in q4:
        item.start()

    def add3(b):
        v = acc2[b, ours, :]
        for d in range(ny - 1):
            v += recv3[d, b].astype(f32)
        slots4[z, b] = v.astype(bf16)

    p4 = []
    for k in range(len(chunks)):
        for item in p3[k]:
            item.wait()
        each(chunks[k], add3)
        group = [
            remote(
                slots4.at[z, part(k)],
                slots4.at[z, part(k)],
                sem_s.at[k, 6 + d],
                sem_r.at[k, 6 + d],
                at_z(d),
            )
            for d in range(1, nz)
        ]
        for item in group:
            item.start()
        p4.append(group)

    def add4(b):
        v = (slots4[0, b].astype(f32) + slots4[1, b].astype(f32)) + (
            slots4[2, b].astype(f32) + slots4[3, b].astype(f32)
        )
        half[b, place, :] = v.astype(bf16)

    p5 = []
    for k in range(len(chunks)):
        for item in p4[k]:
            item.wait()
        each(chunks[k], add4)
        spot = half.at[part(k), place, :]
        group = [
            remote(spot, spot, sem_s.at[k, 9 + d], sem_r.at[k, 9 + d], at_second(d))
            for d in range(1, ny)
        ]
        for item in group:
            item.start()
        p5.append(group)

    for item in q4:
        item.wait()
    total_ref[...] = ((z_s[0] + z_s[1]) + (z_s[2] + z_s[3])) * scale

    p6 = []
    p7 = []
    for k in range(len(chunks)):
        for item in p5[k]:
            item.wait()
        spot = half.at[part(k), mine, :]
        group = [
            remote(spot, spot, sem_s.at[k, 12 + d], sem_r.at[k, 12 + d], at_first(d))
            for d in range(1, nx)
        ]
        for item in group:
            item.start()
        p6.append(group)
        p7.append(
            remote(
                half.at[part(k), mine, :],
                other.at[part(k), mine, :],
                sem_s.at[k, 16],
                sem_r.at[k, 16],
                at_pair(),
            )
        )
        p7[-1].start()
    for k in range(len(chunks)):
        for d in range(1, nx):
            p6[k][d - 1].wait()
            source = lax.rem(first + nx - d, nx)
            rows_d = pl.ds(pl.multiple_of(source * quarter, quarter), quarter)
            p7.append(
                remote(
                    half.at[part(k), rows_d, :],
                    other.at[part(k), rows_d, :],
                    sem_s.at[k, 16 + d],
                    sem_r.at[k, 16 + d],
                    at_pair(),
                )
            )
            p7[-1].start()
    for item in p7:
        item.wait()


def unpack_kernel(scale, core_ref, half_ref, other_ref, small_ref, conv_ref, map_ref, hid_ref, bias_ref, in_ref, out_ref):
    f32 = jnp.float32
    blocks, rows, lanes = half_ref.shape
    width = in_ref.shape[1]

    def write(ref, lane0):
        def conv_out(b, carry):
            lane = pl.ds(pl.multiple_of(lane0, lanes), lanes)
            conv_ref[b, :, lane] = ref[b].astype(f32) * scale
            return carry

        lax.fori_loop(0, 9, conv_out, 0)
        for k in range(4):
            lane = pl.ds(pl.multiple_of(k * rows + lane0, lanes), lanes)
            map_ref[:, lane] = ref[9 + k].astype(f32) * scale
            lane = pl.ds(pl.multiple_of(k % 2 * rows + lane0, lanes), lanes)
            hid_ref[k // 2 * rows : (k // 2 + 1) * rows, lane] = ref[13 + k].astype(f32) * scale

    core = core_ref[0]
    write(half_ref, core * lanes)
    write(other_ref, (1 - core) * lanes)
    bias_ref[...] = small_ref[0:1, :]
    in_ref[0:1, :] = small_ref[1:2, 0:width]
    in_ref[1:2, :] = small_ref[1:2, width:]
    in_ref[2:3, :] = small_ref[2:3, 0:width]
    out_ref[...] = small_ref[2:3, width:]


def run_unpack(half, other, small, scale, width):
    f32 = jnp.float32
    _, ch, _ = half.shape
    core = lax.rem(lax.axis_index("lat"), 2).astype(jnp.int32).reshape(1)
    vmem = pl.BlockSpec(memory_space=pltpu.VMEM)
    return pl.pallas_call(
        functools.partial(unpack_kernel, scale),
        out_shape=(
            jax.ShapeDtypeStruct((9, ch, ch), f32),
            jax.ShapeDtypeStruct((ch, 2 * width), f32),
            jax.ShapeDtypeStruct((width, width), f32),
            jax.ShapeDtypeStruct((1, 2 * width), f32),
            jax.ShapeDtypeStruct((3, width), f32),
            jax.ShapeDtypeStruct((1, width), f32),
        ),
        in_specs=[pl.BlockSpec(memory_space=pltpu.SMEM)] + [vmem] * 3,
        out_specs=(vmem,) * 6,
        compiler_params=pltpu.CompilerParams(vmem_limit_bytes=24 << 20),
        name="unpack",
    )(core, half, other, small)


def run_finish(fg, conv_weight, grads, small, tile_shape, scale, width):
    rows, cols, ch = tile_shape
    f32 = jnp.float32
    bf16 = jnp.bfloat16
    blocks, size, _ = grads.shape
    lanes = size // 2
    nx, ny, nz = 4, 4, 4
    dma = pltpu.SemaphoreType.DMA
    vmem = pl.BlockSpec(memory_space=pltpu.VMEM)
    return pl.pallas_call(
        functools.partial(finish_kernel, (nx, ny, nz), CHUNKS, scale),
        out_shape=(
            jax.ShapeDtypeStruct((rows, cols, ch), f32),
            jax.ShapeDtypeStruct((blocks, size, lanes), bf16),
            jax.ShapeDtypeStruct((blocks, size, lanes), bf16),
            jax.ShapeDtypeStruct(small.shape, f32),
        ),
        in_specs=[vmem] * 4,
        out_specs=(vmem,) * 4,
        scratch_shapes=[
            pltpu.VMEM((blocks, size, lanes), bf16),
            pltpu.VMEM((blocks, size, lanes), bf16),
            pltpu.VMEM((blocks, size, lanes), f32),
            pltpu.VMEM((blocks, size, lanes), bf16),
            pltpu.VMEM((nx - 1, blocks, size // nx, lanes), bf16),
            pltpu.VMEM((blocks, size // nx, lanes), f32),
            pltpu.VMEM((blocks, size // nx, lanes), bf16),
            pltpu.VMEM((ny - 1, blocks, size // nx // ny, lanes), bf16),
            pltpu.VMEM((nz, blocks, size // nx // ny, lanes), bf16),
            pltpu.VMEM((2,) + small.shape, f32),
            pltpu.VMEM((nx,) + small.shape, f32),
            pltpu.VMEM((ny,) + small.shape, f32),
            pltpu.VMEM((nz,) + small.shape, f32),
            pltpu.VMEM((6, cols, ch), bf16),
            pltpu.VMEM((2, rows, ch), bf16),
            pltpu.VMEM((2, rows, ch), bf16),
            dma((len(CHUNKS), 20)),
            dma((len(CHUNKS), 20)),
            dma((10,)),
            dma((10,)),
            dma((8,)),
            dma((8,)),
        ],
        compiler_params=pltpu.CompilerParams(
            vmem_limit_bytes=48 << 20, collective_id=1, has_side_effects=True
        ),
        name="finish",
    )(fg, conv_weight, grads, small)


def on_device(
    latents,
    conv_weight,
    map_weight,
    map_bias,
    input_weight,
    hidden_weight,
    output_weight,
    hit_owner,
    serve_block,
    query_grid,
    cotangent,
):
    rows, cols, ch = latents.shape
    lat_parts = lax.axis_size("lat")
    lon_parts = lax.axis_size("lon")
    dev_count = lat_parts * lon_parts
    dims = (rows * lat_parts, cols * lon_parts)
    hits = hit_owner.shape[0]
    group = cotangent.shape[0] // hits
    f32 = jnp.float32

    grid = query_grid.astype(f32).reshape(3, hits, group)
    data = jnp.concatenate(
        [grid[0], grid[1], grid[2], cotangent.reshape(hits, group)], axis=1
    )
    arrived, *halo = run_front(data, hit_owner, latents, lat_parts, lon_parts)
    arrived = arrived.reshape(dev_count, 4, group)
    block = jnp.maximum(serve_block[0], 0).astype(f32)[:, None]
    sub = arrived[:, 1]
    sub_r = jnp.floor((sub + 0.5) * (1.0 / SUB))
    zero = jnp.zeros_like(sub)
    queries = jnp.stack(
        [
            arrived[:, 0] + BLOCK * block,
            sub_r,
            sub - SUB * sub_r,
            arrived[:, 2],
            arrived[:, 3],
            zero,
            zero,
            zero,
        ]
    ).reshape(8, dev_count * group)

    base = jnp.stack(
        [lax.axis_index("lat") * rows, lax.axis_index("lon") * cols]
    ).astype(f32)
    weights = (conv_weight, map_weight, map_bias, input_weight, hidden_weight, output_weight)
    fg, grads, small = run_main(base, queries, latents, halo, weights, dims)
    scale = float(hits * group * dev_count) ** (-0.5)
    width = input_weight.shape[1]
    latent_grad, half, other, small = run_finish(
        fg, conv_weight, grads, small, latents.shape, scale, width
    )
    conv_grad, map_grad, hidden_grad, bias_grad, input_grad, output_grad = run_unpack(
        half, other, small, scale, width
    )
    return (
        latent_grad,
        conv_grad,
        map_grad,
        bias_grad[0],
        input_grad,
        hidden_grad[None],
        output_grad[0],
    )


def solution(mesh):
    placed = (
        P("lat", "lon", None),
        P(),
        P(),
        P(),
        P(),
        P(),
        P(),
        P(("lat", "lon")),
        P(("lat", "lon"), None),
        P(None, ("lat", "lon")),
        P(("lat", "lon")),
    )
    return jax.shard_map(
        on_device,
        mesh=mesh,
        in_specs=placed,
        out_specs=(P("lat", "lon", None), P(), P(), P(), P(), P(), P()),
        check_vma=False,
    )
```

time: 149 us -> 118 us (0.79)
  starting transfers between devices: 21.5 us -> 0 us
  local copies, waits for them, and re-layouts: 10.3 us -> 4.43 us
  waiting for transfers between devices: 3.36 us -> 0 us
    ppermute x4 -> x0, starting transfers between devices: 11.8 us -> none  [the longest x1 3.53 us: halo_of(): top = lax.ppermute(tile[-1:], 'lat', up)]
    pallas_call x1, Pallas kernels: 60.2 us -> 49.8 us  [run_main(): pl.pallas_call(functools.partial(main_kernel, dims), out_shape=(jax.Shape...]
    pallas_call x1 -> x3, Pallas kernels: 49.4 us -> 59.6 us  [the longest x1 39 us: run_finish(): pl.pallas_call(functools.partial(finish_kernel, (nx, ny, nz), CHUNKS, sca...]
    all_to_all x1 -> x0, starting transfers between devices: 9.65 us -> none  [on_device(): lax.all_to_all(outgoing.reshape(dev_count, 1, 4 * group), ('lat', 'lon'),...]
    all_to_all x1 -> x0, waiting for transfers between devices: 3.35 us -> none  [on_device(): lax.all_to_all(outgoing.reshape(dev_count, 1, 4 * group), ('lat', 'lon'),...]
    slice x7 -> x0, local copies, waits for them, and re-layouts: 3.22 us -> none  [the longest x1 0.9 us: column(): tile[:, j]]
    unnamed x20 -> x19, local copies, waits for them, and re-layouts: 4.09 us -> 2.29 us
  transfers between devices with their start and end apart: 5 -> 0, of which waited for: 1 -> 0; matrix products, arithmetic and copies ran while one was open for 5% -> 0% of each run, Pallas kernels for 0% -> 0%
where the time goes in v3:
time: 118 us; the launch traced here: 117 us
  Pallas kernels  109 us (92%)
  local copies, waits for them, and re-layouts  4.43 us (4%)
  other arithmetic  2.63 us (2%)
    pallas_call x1, Pallas kernels, run_main(): pl.pallas_call(functools.partial(main_kernel, dims), out_shape=(jax.Shape...  49.8 us
    pallas_call x1, Pallas kernels, run_finish(): pl.pallas_call(functools.partial(finish_kernel, (nx, ny, nz), CHUNKS, sca...  39 us
    pallas_call x1, Pallas kernels, run_front(): pl.pallas_call(front_kernel, out_shape=(jax.ShapeDtypeStruct((lat_n, lon_...  18 us
    pallas_call x1, Pallas kernels, run_unpack(): pl.pallas_call(functools.partial(unpack_kernel, scale), out_shape=(jax.Sh...  2.61 us

profile of v3, /device:TPU:1, one launch (start us, length us, event | category | flops | bytes accessed | tf_op | source)
XLA Modules:
  0.0 117.4 jit_solution(9309887576664691872)
XLA Ops:
  0.6 0.1 add_convert_fusion.base_ref
  0.7 0.7 multiply_bitcast_fusion
  1.4 0.8 reshape.128
  2.2 0.9 convert_element_type.15
  3.1 0.2 slice_reduce_fusion.5
  3.3 0.1 squeeze.23
  3.4 0.1 squeeze.25
  3.4 0.1 squeeze.24
  3.5 0.1 pad_maximum_fusion.data_ref
  3.6 0.9 copy-done.3
  4.5 0.7 copy-done.8
  5.2 18.0 %front.1 = (f32[8,16,256]{2,1,0:T(8,128)S(1)}, bf16[16,256]{1,0:T(8,128)(2,1)S(1)}, bf16[16,256]{1,0:T(8,128)(2,1)S(1)}, bf16[18,256]{1,0:T(8,128)(2,1)S(1)}, bf16[18,256]{1,0:T(8,128)(2,1)S(1)}) custom-call(f32[96,256]{1,0:T(8,128)S(1)} %pad_maximum_fusion.data_ref, s32[1,96]{1,0:T(1,128)S(1)} %bitcast.19, bf16[256,256]{1,0:T(8,128)(2,1)S(1)} %bitcast.16), custom_call_target="tpu_custom_call" | custom-call | tf_op jit(solution)/shard_map/front/pallas_call | solution.py:582
  23.2 0.2 reshape.131
  23.4 0.8 slice_reduce_fusion
  24.2 0.1 stack.26
  24.3 0.1 stack.25
  24.4 0.1 squeeze.26
  24.5 0.1 add.40
  24.6 0.1 multiply_subtract_fusion
  24.8 0.3 stack.28.q_ref
  25.2 49.8 %queries.1 = (bf16[256,256]{1,0:T(8,128)(2,1)S(1)}, f32[17,256,256]{2,1,0:T(8,128)}, f32[8,1024]{1,0:T(8,128)S(1)}) custom-call(f32[2]{0:T(128)S(1)} %add_convert_fusion.base_ref, f32[8,8192]{1,0:T(8,128)S(1)} %stack.28.q_ref, bf16[16,16,256]{2,1,0:T(8,128)(2,1)S(1)} %copy-done.4, bf16[16,256]{1,0:T(8,128)(2,1)S(1)} %get-tuple-element.26.top_ref, ...), custom_call_target="tpu_custom_call" | custom-call | tf_op jit(solution)/shard_map/queries/pallas_call | solution.py:382
  75.0 39.0 %finish.1 = (f32[16,16,256]{2,1,0:T(8,128)S(1)}, bf16[17,256,128]{2,1,0:T(8,128)(2,1)S(1)}, bf16[17,256,128]{2,1,0:T(8,128)(2,1)S(1)}, f32[8,1024]{1,0:T(8,128)S(1)}) custom-call(bf16[256,256]{1,0:T(8,128)(2,1)S(1)} %get-tuple-element.30.fg_ref, bf16[9,256,256]{2,1,0:T(8,128)(2,1)S(1)} %copy-done, f32[17,256,256]{2,1,0:T(8,128)} %get-tuple-element.31.wg_ref, ...), custom_call_target="tpu_custom_call" | custom-call | tf_op jit(solution)/shard_map/finish/pallas_call | solution.py:967
  114.0 2.6 %unpack.1 = (f32[9,256,256]{2,1,0:T(8,128)}, f32[256,1024]{1,0:T(8,128)}, f32[512,512]{1,0:T(8,128)}, f32[1,1024]{1,0:T(1,128)}, f32[3,512]{1,0:T(4,128)}, /*index=5*/f32[1,512]{1,0:T(1,128)}) custom-call(s32[1]{0:T(128)} %bitcast.9.core_ref, bf16[17,256,128]{2,1,0:T(8,128)(2,1)S(1)} %get-tuple-element.34.half_ref, ...), custom_call_target="tpu_custom_call" | custom-call | tf_op jit(solution)/shard_map/unpack/pallas_call | solution.py:941
  116.7 0.7 copy.23
  (18 shorter events, 0.1 us)
Async XLA Ops:
  3.5 21.6 %copy-start.4 = (bf16[16,16,256]{2,1,0:T(8,128)(2,1)S(1)}, bf16[16,16,256]{2,1,0:T(8,128)(2,1)}, u32[]{:S(2)}) copy-start(bf16[16,16,256]{2,1,0:T(8,128)(2,1)} %center_ref.1) | copy-start | bytes 393220
  3.6 0.9 copy-start.3
  4.5 0.7 copy-start.8
  5.2 19.9 %copy-start = (bf16[9,256,256]{2,1,0:T(8,128)(2,1)S(1)}, bf16[9,256,256]{2,1,0:T(8,128)(2,1)}, u32[]{:S(2)}) copy-start(bf16[9,256,256]{2,1,0:T(8,128)(2,1)} %convw_ref.1) | copy-start | bytes 3538948
  5.2 19.9 %copy-start.1 = (bf16[256,1024]{1,0:T(8,128)(2,1)S(1)}, bf16[256,1024]{1,0:T(8,128)(2,1)}, u32[]{:S(2)}) copy-start(bf16[256,1024]{1,0:T(8,128)(2,1)} %mapw_ref.1) | copy-start | bytes 1572868
  5.2 19.9 %copy-start.2 = (bf16[1,512,512]{2,1,0:T(8,128)(2,1)S(1)}, bf16[1,512,512]{2,1,0:T(8,128)(2,1)}, u32[]{:S(2)}) copy-start(bf16[1,512,512]{2,1,0:T(8,128)(2,1)} %param.16) | copy-start | bytes 1572868
  5.2 19.9 %copy-start.5 = (f32[3,512]{1,0:T(4,128)S(1)}, f32[3,512]{1,0:T(4,128)}, u32[]{:S(2)}) copy-start(f32[3,512]{1,0:T(4,128)} %inw_ref.1) | copy-start | bytes 18436
  5.2 19.9 %copy-start.6 = (f32[1024]{0:T(1024)S(1)}, f32[1024]{0:T(1024)}, u32[]{:S(2)}) copy-start(f32[1024]{0:T(1024)} %param.14) | copy-start | bytes 12292
  5.2 19.9 %copy-start.7 = (f32[512]{0:T(512)S(1)}, f32[512]{0:T(512)}, u32[]{:S(2)}) copy-start(f32[512]{0:T(512)} %param.17) | copy-start | bytes 6148

commit v4 on v3

--- a/solution.py
+++ b/solution.py
@@ -21,21 +21,26 @@
 NCH = 256
 GM = 272
 SPLIT = 10
+MAIN_MB = 36
+FINISH_MB = 24
 CHUNKS = ((0, 6), (6, 12), (12, 17))
 
 
 def _fit():
     nodes = np.cos((2 * np.arange(400) + 1) * np.pi / 800)
     r = (nodes + 1) / 4
-    z = r * r
-    sine = np.sqrt(2.0) * np.sin(np.pi * r)
-    cosine = np.sqrt(2.0) * np.cos(np.pi * r)
-    sa = np.stack([r * z**k for k in range(4)], 1)
-    ca = np.stack([z**k for k in range(5)], 1)
-    return (
-        [float(v) for v in np.linalg.lstsq(sa, sine, rcond=None)[0]],
-        [float(v) for v in np.linalg.lstsq(ca, cosine, rcond=None)[0]],
-    )
+    found = []
+    for odd, target in ((1, np.sin(np.pi * r)), (0, np.cos(np.pi * r))):
+        basis = np.stack([r ** (2 * k + odd) for k in range(4)], 1)
+        target = np.sqrt(2.0) * target
+        weight = np.ones(len(r))
+        for _ in range(60):
+            root = np.sqrt(weight)
+            c = np.linalg.lstsq(basis * root[:, None], target * root, rcond=None)[0]
+            weight = weight * np.abs(basis @ c - target)
+            weight = weight / weight.sum()
+        found.append([float(np.float32(v)) for v in c])
+    return found
 
 
 SIN_C, COS_C = _fit()
@@ -45,7 +50,7 @@
     r = t - jnp.round(t)
     z = r * r
     s = r * (SIN_C[0] + z * (SIN_C[1] + z * (SIN_C[2] + z * SIN_C[3])))
-    c = COS_C[0] + z * (COS_C[1] + z * (COS_C[2] + z * (COS_C[3] + z * COS_C[4])))
+    c = COS_C[0] + z * (COS_C[1] + z * (COS_C[2] + z * COS_C[3]))
     return s * c, 1.0 - s * s
 
 
@@ -183,10 +188,12 @@
     def encode(k, at):
         k = k % 4
         rhs_ref = rhs_refs[k]
-        cell_q = q_ref[0:1, at]
+        cell_q = q_ref[0:1, at].astype(bf16)
+        one = jnp.ones((64, tile), bf16)
+        zero = jnp.zeros((64, tile), bf16)
         for m in range(0, cells, 64):
-            iota = (lax.broadcasted_iota(jnp.int32, (64, tile), 0) + m).astype(f32)
-            onehot = jnp.where(iota == cell_q, 1.0, 0.0).astype(bf16)
+            iota = (lax.broadcasted_iota(jnp.int32, (64, tile), 0) + m).astype(f32).astype(bf16)
+            onehot = jnp.where(iota == cell_q, one, zero)
             rhs_ref[oh0 + m : oh0 + m + 64, :] = onehot
             rhs_ref[oh1 + m : oh1 + m + 64, :] = onehot
         r = lax.broadcasted_iota(jnp.int32, (16, tile), 0)
@@ -402,7 +409,7 @@
         + [pltpu.VMEM((width, TILE), f32)] * 4
         + [pltpu.VMEM((2 * width, TILE), bf16)] * 4
         + [pltpu.VMEM((width, TILE), f32)] * 3,
-        compiler_params=pltpu.CompilerParams(vmem_limit_bytes=48 << 20),
+        compiler_params=pltpu.CompilerParams(vmem_limit_bytes=MAIN_MB << 20),
         name="queries",
     )(
         base,
@@ -490,7 +497,8 @@
 
 
 def front_kernel(
-    data_ref,
+    grid_ref,
+    cot_ref,
     owner_ref,
     tile_ref,
     out_ref,
@@ -498,6 +506,7 @@
     bottom_ref,
     left_ref,
     right_ref,
+    data,
     go,
     mid,
     turned,
@@ -512,7 +521,7 @@
     lat = lax.axis_index("lat")
     lon = lax.axis_index("lon")
     lat_n, lon_n, words = out_ref.shape
-    hits = data_ref.shape[0]
+    hits, group = cot_ref.shape
     cols = top_ref.shape[0]
     rows = tile_ref.shape[0] // cols
 
@@ -528,8 +537,11 @@
     at = lax.broadcasted_iota(jnp.int32, (lat_n * lon_n, hits), 0)
     device = lax.rem(at, lat_n) * lon_n + lax.div(at, lat_n)
     pick = jnp.where(device == owner_ref[...], 1.0, 0.0).astype(jnp.float32)
+    for k in range(3):
+        data[:, k * group : (k + 1) * group] = grid_ref[k].astype(jnp.float32)
+    data[:, 3 * group :] = cot_ref[...]
     picked = jnp.dot(
-        pick, data_ref[...], precision=lax.Precision.HIGHEST, preferred_element_type=jnp.float32
+        pick, data[...], precision=lax.Precision.HIGHEST, preferred_element_type=jnp.float32
     )
     go[...] = picked.reshape(lon_n, lat_n, words)
     mid[lon] = go[lon]
@@ -572,9 +584,10 @@
         item.wait()
 
 
-def run_front(data, owner, tile, lat_n, lon_n):
+def run_front(grid, cot, owner, tile, lat_n, lon_n):
     rows, cols, ch = tile.shape
-    hits, words = data.shape
+    hits, group = cot.shape
+    words = 4 * group
     f32 = jnp.float32
     bf16 = jnp.bfloat16
     dma = pltpu.SemaphoreType.DMA
@@ -588,9 +601,10 @@
             jax.ShapeDtypeStruct((rows + 2, ch), bf16),
             jax.ShapeDtypeStruct((rows + 2, ch), bf16),
         ),
-        in_specs=[vmem] * 3,
+        in_specs=[vmem] * 4,
         out_specs=(vmem,) * 5,
         scratch_shapes=[
+            pltpu.VMEM((hits, words), f32),
             pltpu.VMEM((lon_n, lat_n, words), f32),
             pltpu.VMEM((lon_n, lat_n, words), f32),
             pltpu.VMEM((lat_n, lon_n, words), f32),
@@ -606,7 +620,7 @@
             vmem_limit_bytes=16 << 20, collective_id=2, has_side_effects=True
         ),
         name="front",
-    )(data, owner.reshape(1, hits), tile.reshape(rows * cols, ch))
+    )(grid, cot, owner.reshape(1, hits), tile.reshape(rows * cols, ch))
 
 
 def finish_kernel(
@@ -667,14 +681,8 @@
     def at_z(d):
         return (lax.rem(z + d, nz) * 2 + c, lon)
 
-    def at_first(d):
-        return (lat, (1 - c) * at_x(d)[1] + c * at_y(d)[1])
-
-    def at_second(d):
-        return (lat, c * at_x(d)[1] + (1 - c) * at_y(d)[1])
-
-    first = (1 - c) * x + c * y
-    second = c * x + (1 - c) * y
+    axes = ((x, nx, at_x), (y, ny, at_y), (z, nz, at_z))
+    orders = [[axes[(k + j) % 3] for j in range(3)] for k in range(len(chunks))]
 
     peers = [at_pair()]
     peers += [at_x(d) for d in range(1, nx)]
@@ -687,9 +695,13 @@
     cells = tile_rows * cols
     keep = pl.ds(pl.multiple_of(c * lanes, lanes), lanes)
     give = pl.ds(pl.multiple_of((1 - c) * lanes, lanes), lanes)
-    mine = pl.ds(pl.multiple_of(first * quarter, quarter), quarter)
-    ours = pl.ds(pl.multiple_of(second * final, final), final)
-    place = pl.ds(pl.multiple_of(first * quarter + second * final, final), final)
+
+    def span(start, size):
+        return pl.ds(pl.multiple_of(start, size), size)
+
+    mine = [span(o[0][0] * quarter, quarter) for o in orders]
+    ours = [span(o[1][0] * final, final) for o in orders]
+    place = [span(o[0][0] * quarter + o[1][0] * final, final) for o in orders]
 
     def each(chunk, body):
         def one(b, carry):
@@ -741,8 +753,9 @@
         p1[k].wait()
         each(chunks[k], add1)
         group = []
-        for d in range(1, nx):
-            target = lax.rem(first + d, nx)
+        pos, count, at_first = orders[k][0]
+        for d in range(1, count):
+            target = lax.rem(pos + d, count)
             group.append(
                 remote(
                     send2.at[part(k), pl.ds(pl.multiple_of(target * quarter, quarter), quarter), :],
@@ -777,8 +790,8 @@
             acc = piece if acc is None else acc + piece
     latent_ref[...] = acc.reshape(tile_rows, cols, ch)
 
-    def add2(b):
-        v = acc1[b, mine, :]
+    def add2(k, b):
+        v = acc1[b, mine[k], :]
         for d in range(nx - 1):
             v += recv2[d, b].astype(f32)
         acc2[b] = v
@@ -788,10 +801,11 @@
     for k in range(len(chunks)):
         for item in p2[k]:
             item.wait()
-        each(chunks[k], add2)
+        each(chunks[k], functools.partial(add2, k))
         group = []
-        for d in range(1, ny):
-            target = lax.rem(second + d, ny)
+        pos, count, at_second = orders[k][1]
+        for d in range(1, count):
+            target = lax.rem(pos + d, count)
             group.append(
                 remote(
                     send3.at[part(k), pl.ds(pl.multiple_of(target * final, final), final), :],
@@ -814,46 +828,42 @@
     for item in q4:
         item.start()
 
-    def add3(b):
-        v = acc2[b, ours, :]
+    def add3(k, b):
+        v = acc2[b, ours[k], :]
         for d in range(ny - 1):
             v += recv3[d, b].astype(f32)
-        slots4[z, b] = v.astype(bf16)
+        slots4[orders[k][2][0], b] = v.astype(bf16)
 
     p4 = []
     for k in range(len(chunks)):
         for item in p3[k]:
             item.wait()
-        each(chunks[k], add3)
+        each(chunks[k], functools.partial(add3, k))
+        pos, count, at_third = orders[k][2]
+        spot = slots4.at[pos, part(k)]
         group = [
-            remote(
-                slots4.at[z, part(k)],
-                slots4.at[z, part(k)],
-                sem_s.at[k, 6 + d],
-                sem_r.at[k, 6 + d],
-                at_z(d),
-            )
-            for d in range(1, nz)
+            remote(spot, spot, sem_s.at[k, 6 + d], sem_r.at[k, 6 + d], at_third(d))
+            for d in range(1, count)
         ]
         for item in group:
             item.start()
         p4.append(group)
 
-    def add4(b):
+    def add4(k, b):
         v = (slots4[0, b].astype(f32) + slots4[1, b].astype(f32)) + (
             slots4[2, b].astype(f32) + slots4[3, b].astype(f32)
         )
-        half[b, place, :] = v.astype(bf16)
+        half[b, place[k], :] = v.astype(bf16)
 
     p5 = []
     for k in range(len(chunks)):
         for item in p4[k]:
             item.wait()
-        each(chunks[k], add4)
-        spot = half.at[part(k), place, :]
+        each(chunks[k], functools.partial(add4, k))
+        spot = half.at[part(k), place[k], :]
         group = [
-            remote(spot, spot, sem_s.at[k, 9 + d], sem_r.at[k, 9 + d], at_second(d))
-            for d in range(1, ny)
+            remote(spot, spot, sem_s.at[k, 9 + d], sem_r.at[k, 9 + d], orders[k][1][2](d))
+            for d in range(1, orders[k][1][1])
         ]
         for item in group:
             item.start()
@@ -868,18 +878,18 @@
     for k in range(len(chunks)):
         for item in p5[k]:
             item.wait()
-        spot = half.at[part(k), mine, :]
+        spot = half.at[part(k), mine[k], :]
         group = [
-            remote(spot, spot, sem_s.at[k, 12 + d], sem_r.at[k, 12 + d], at_first(d))
-            for d in range(1, nx)
+            remote(spot, spot, sem_s.at[k, 12 + d], sem_r.at[k, 12 + d], orders[k][0][2](d))
+            for d in range(1, orders[k][0][1])
         ]
         for item in group:
             item.start()
         p6.append(group)
         p7.append(
             remote(
-                half.at[part(k), mine, :],
-                other.at[part(k), mine, :],
+                half.at[part(k), mine[k], :],
+                other.at[part(k), mine[k], :],
                 sem_s.at[k, 16],
                 sem_r.at[k, 16],
                 at_pair(),
@@ -887,10 +897,10 @@
         )
         p7[-1].start()
     for k in range(len(chunks)):
-        for d in range(1, nx):
+        pos, count, _ = orders[k][0]
+        for d in range(1, count):
             p6[k][d - 1].wait()
-            source = lax.rem(first + nx - d, nx)
-            rows_d = pl.ds(pl.multiple_of(source * quarter, quarter), quarter)
+            rows_d = span(lax.rem(pos + count - d, count) * quarter, quarter)
             p7.append(
                 remote(
                     half.at[part(k), rows_d, :],
@@ -999,7 +1009,7 @@
             dma((8,)),
         ],
         compiler_params=pltpu.CompilerParams(
-            vmem_limit_bytes=48 << 20, collective_id=1, has_side_effects=True
+            vmem_limit_bytes=FINISH_MB << 20, collective_id=1, has_side_effects=True
         ),
         name="finish",
     )(fg, conv_weight, grads, small)
@@ -1027,11 +1037,14 @@
     group = cotangent.shape[0] // hits
     f32 = jnp.float32
 
-    grid = query_grid.astype(f32).reshape(3, hits, group)
-    data = jnp.concatenate(
-        [grid[0], grid[1], grid[2], cotangent.reshape(hits, group)], axis=1
+    arrived, *halo = run_front(
+        query_grid.reshape(3, hits, group),
+        cotangent.reshape(hits, group),
+        hit_owner,
+        latents,
+        lat_parts,
+        lon_parts,
     )
-    arrived, *halo = run_front(data, hit_owner, latents, lat_parts, lon_parts)
     arrived = arrived.reshape(dev_count, 4, group)
     block = jnp.maximum(serve_block[0], 0).astype(f32)[:, None]
     sub = arrived[:, 1]

time: 118 us -> 109 us (0.924)
  Pallas kernels: 109 us -> 101 us
    pallas_call x1, Pallas kernels: 49.8 us -> 45.7 us  [run_main(): pl.pallas_call(functools.partial(main_kernel, dims), out_shape=(jax.Shape...]
    pallas_call x1, Pallas kernels: 39 us -> 34.9 us  [run_finish(): pl.pallas_call(functools.partial(finish_kernel, (nx, ny, nz), CHUNKS, sca...]
where the time goes in v4:
time: 109 us
  Pallas kernels  101 us (93%)
  local copies, waits for them, and re-layouts  5.06 us (5%)
  other arithmetic  1.62 us (1%)
    pallas_call x1, Pallas kernels, run_main(): pl.pallas_call(functools.partial(main_kernel, dims), out_shape=(jax.Shape...  45.7 us
    pallas_call x1, Pallas kernels, run_finish(): pl.pallas_call(functools.partial(finish_kernel, (nx, ny, nz), CHUNKS, sca...  34.9 us
    pallas_call x1, Pallas kernels, run_front(): pl.pallas_call(front_kernel, out_shape=(jax.ShapeDtypeStruct((lat_n, lon_...  18 us
    pallas_call x1, Pallas kernels, run_unpack(): pl.pallas_call(functools.partial(unpack_kernel, scale), out_shape=(jax.Sh...  2.61 us
    unnamed x19, local copies, waits for them, and re-layouts  2.3 us

profile of v4, /device:TPU:1, one launch (start us, length us, event | category | flops | bytes accessed | tf_op | source)
XLA Modules:
  0.0 108.7 jit_solution(2387580090938831635)
XLA Ops:
  0.6 0.1 add_convert_fusion.base_ref
  0.7 0.7 multiply_bitcast_fusion
  1.4 0.8 reshape.125.cot_ref
  2.2 1.0 reshape.124.grid_ref
  3.2 0.9 copy-done.3
  4.1 0.7 copy-done.8
  4.8 0.0 copy-start.5
  4.8 0.0 copy-start.6
  4.8 0.0 copy-start.7
  4.8 18.0 %front.1 = (f32[8,16,256]{2,1,0:T(8,128)S(1)}, bf16[16,256]{1,0:T(8,128)(2,1)S(1)}, bf16[16,256]{1,0:T(8,128)(2,1)S(1)}, bf16[18,256]{1,0:T(8,128)(2,1)S(1)}, bf16[18,256]{1,0:T(8,128)(2,1)S(1)}) custom-call(s32[3,96,64]{2,1,0:T(8,128)S(1)} %reshape.124.grid_ref, f32[96,64]{1,0:T(8,128)S(1)} %reshape.125.cot_ref, s32[1,96]{1,0:T(1,128)S(1)} %bitcast.19, ...), custom_call_target="tpu_custom_call" | custom-call | tf_op jit(solution)/shard_map/front/pallas_call | solution.py:595
  22.8 0.2 reshape.128
  23.0 0.8 slice_reduce_fusion
  23.8 0.1 stack.26
  23.9 0.1 stack.25
  24.0 0.1 squeeze.14
  24.1 0.1 add.40
  24.2 0.1 multiply_subtract_fusion
  24.4 0.3 stack.28.q_ref
  24.7 0.0 copy-done
  24.7 0.0 copy-done.1
  24.8 45.7 %queries.1 = (bf16[256,256]{1,0:T(8,128)(2,1)S(1)}, f32[17,256,256]{2,1,0:T(8,128)S(1)}, f32[8,1024]{1,0:T(8,128)S(1)}) custom-call(f32[2]{0:T(128)S(1)} %add_convert_fusion.base_ref, f32[8,8192]{1,0:T(8,128)S(1)} %stack.28.q_ref, bf16[16,16,256]{2,1,0:T(8,128)(2,1)S(1)} %copy-done.4, bf16[16,256]{1,0:T(8,128)(2,1)S(1)} %get-tuple-element.26.top_ref, ...), custom_call_target="tpu_custom_call" | custom-call | tf_op jit(solution)/shard_map/queries/pallas_call | solution.py:389
  70.4 34.9 %finish.1 = (f32[16,16,256]{2,1,0:T(8,128)S(1)}, bf16[17,256,128]{2,1,0:T(8,128)(2,1)S(1)}, bf16[17,256,128]{2,1,0:T(8,128)(2,1)S(1)}, f32[8,1024]{1,0:T(8,128)S(1)}) custom-call(bf16[256,256]{1,0:T(8,128)(2,1)S(1)} %get-tuple-element.30.fg_ref, bf16[9,256,256]{2,1,0:T(8,128)(2,1)S(1)} %copy-done, f32[17,256,256]{2,1,0:T(8,128)S(1)} %get-tuple-element.31.wg_ref, ...), custom_call_target="tpu_custom_call" | custom-call | tf_op jit(solution)/shard_map/finish/pallas_call | solution.py:977
  105.4 2.6 %unpack.1 = (f32[9,256,256]{2,1,0:T(8,128)}, f32[256,1024]{1,0:T(8,128)}, f32[512,512]{1,0:T(8,128)}, f32[1,1024]{1,0:T(1,128)}, f32[3,512]{1,0:T(4,128)}, /*index=5*/f32[1,512]{1,0:T(1,128)}) custom-call(s32[1]{0:T(128)} %bitcast.9.core_ref, bf16[17,256,128]{2,1,0:T(8,128)(2,1)S(1)} %get-tuple-element.34.half_ref, ...), custom_call_target="tpu_custom_call" | custom-call | tf_op jit(solution)/shard_map/unpack/pallas_call | solution.py:951
  108.0 0.7 copy.23
  (13 shorter events, 0.1 us)
Async XLA Ops:
  3.2 0.9 copy-start.3
  4.1 0.7 copy-start.8
  4.8 19.9 %copy-start = (bf16[9,256,256]{2,1,0:T(8,128)(2,1)S(1)}, bf16[9,256,256]{2,1,0:T(8,128)(2,1)}, u32[]{:S(2)}) copy-start(bf16[9,256,256]{2,1,0:T(8,128)(2,1)} %convw_ref.1) | copy-start | bytes 3538948
  4.8 19.9 %copy-start.1 = (bf16[256,1024]{1,0:T(8,128)(2,1)S(1)}, bf16[256,1024]{1,0:T(8,128)(2,1)}, u32[]{:S(2)}) copy-start(bf16[256,1024]{1,0:T(8,128)(2,1)} %mapw_ref.1) | copy-start | bytes 1572868
  4.8 19.9 %copy-start.2 = (bf16[1,512,512]{2,1,0:T(8,128)(2,1)S(1)}, bf16[1,512,512]{2,1,0:T(8,128)(2,1)}, u32[]{:S(2)}) copy-start(bf16[1,512,512]{2,1,0:T(8,128)(2,1)} %param.16) | copy-start | bytes 1572868
  4.8 19.9 %copy-start.4 = (bf16[16,16,256]{2,1,0:T(8,128)(2,1)S(1)}, bf16[16,16,256]{2,1,0:T(8,128)(2,1)}, u32[]{:S(2)}) copy-start(bf16[16,16,256]{2,1,0:T(8,128)(2,1)} %center_ref.1) | copy-start | bytes 393220
  4.8 20.0 %copy-start.5 = (f32[3,512]{1,0:T(4,128)S(1)}, f32[3,512]{1,0:T(4,128)}, u32[]{:S(2)}) copy-start(f32[3,512]{1,0:T(4,128)} %inw_ref.1) | copy-start | bytes 18436
  4.8 20.0 %copy-start.6 = (f32[1024]{0:T(1024)S(1)}, f32[1024]{0:T(1024)}, u32[]{:S(2)}) copy-start(f32[1024]{0:T(1024)} %param.14) | copy-start | bytes 12292
  4.8 20.0 %copy-start.7 = (f32[512]{0:T(512)S(1)}, f32[512]{0:T(512)}, u32[]{:S(2)}) copy-start(f32[512]{0:T(512)} %param.17) | copy-start | bytes 6148

commit v5 on v4

--- a/solution.py
+++ b/solution.py
@@ -96,7 +96,6 @@
 
 def main_kernel(
     dims,
-    base_ref,
     q_ref,
     center_ref,
     top_ref,
@@ -117,7 +116,7 @@
     feat_ref,
     tab0_ref,
     tab1_ref,
-    wcol_ref,
+    hidw_ref,
     g_ref,
     og_ref,
     *pairs,
@@ -145,8 +144,10 @@
     cell = lax.broadcasted_iota(jnp.int32, (cells, width), 0)
     row_f = (cell // cols).astype(f32)
     col_f = (cell % cols).astype(f32)
-    lat_c = ((base_ref[0] + row_f) * SUB + 0.5) * (2.0 / (lat_cells * SUB)) - 1.0
-    lon_c = ((base_ref[1] + col_f) * SUB + 0.5) * (2.0 / (lon_cells * SUB)) - 1.0
+    lat0 = (lax.axis_index("lat") * rows).astype(f32)
+    lon0 = (lax.axis_index("lon") * cols).astype(f32)
+    lat_c = ((lat0 + row_f) * SUB + 0.5) * (2.0 / (lat_cells * SUB)) - 1.0
+    lon_c = ((lon0 + col_f) * SUB + 0.5) * (2.0 / (lon_cells * SUB)) - 1.0
     lev_c = 1.0 / LEVELS - 1.0
     linear = (
         lat_c * inw_ref[0:1, :] + lon_c * inw_ref[1:2, :] + lev_c * inw_ref[2:3, :]
@@ -174,7 +175,7 @@
         for c in range(3):
             ext = jnp.where(ext_row == level * 3 + c, parts[c][level], ext)
     tab0_ref[:, 2 * cells : 2 * cells + 128] = ext.T.astype(bf16)
-    wcol_ref[...] = jnp.broadcast_to(outw_ref[...], (128, width)).T
+    hidw_ref[...] = (hid_ref[...].astype(f32) * outw_ref[...]).astype(bf16)
 
     oh0 = width
     oh1 = width + cells
@@ -226,7 +227,7 @@
     def back_dot(k):
         k = k % 4
 
-        return dots(te_ref, hid_ref, d_refs[k], slice(width, 2 * width))
+        return dots(te_ref, hidw_ref, d_refs[k], slice(width, 2 * width))
 
     def first_sine(k):
         k = k % 4
@@ -250,13 +251,10 @@
                 s, c = sincos_turns(tc_ref[m : m + ROWS, :] * INV_TURN)
                 sw = s * cot
                 cc = c * cot
-                w = wcol_ref[m : m + ROWS, :]
                 og = og_ref[m : m + ROWS, :]
                 for n in range(0, tile, 128):
                     og = og + sw[:, n : n + 128]
-                    d_refs[k][width + m : width + m + ROWS, n : n + 128] = (
-                        cc[:, n : n + 128] * w
-                    ).astype(bf16)
+                d_refs[k][width + m : width + m + ROWS, :] = cc.astype(bf16)
                 og_ref[m : m + ROWS, :] = og
 
             return run
@@ -346,6 +344,8 @@
     for u in range(4):
         stage(u, tiles - 4 + u, 4 - u)
 
+    hidg_ref[...] = hidg_ref[...] * outw_ref[...]
+    g_ref[:, width:] = g_ref[:, width:] * outw_ref[...]
     g = g_ref[0:cells, :]
     hi, lo = split2(g)
     fg = (dot_nt(hi, mapw_ref[...]) + dot_nt(lo, mapw_ref[...])).astype(bf16)
@@ -378,7 +378,7 @@
     small_ref[2:3, width:] = og
 
 
-def run_main(base, queries, center, halo, weights, dims):
+def run_main(queries, center, halo, weights, dims):
     conv_weight, map_weight, map_bias, input_weight, hidden_weight, output_weight = weights
     rows, cols, ch = center.shape
     cells = rows * cols
@@ -393,7 +393,7 @@
             jax.ShapeDtypeStruct((17, ch, ch), f32),
             jax.ShapeDtypeStruct((8, 2 * width), f32),
         ),
-        in_specs=[pl.BlockSpec(memory_space=pltpu.SMEM)] + [vmem] * 12,
+        in_specs=[vmem] * 12,
         out_specs=(vmem,) * 3,
         scratch_shapes=[
             pltpu.VMEM((width, width), f32),
@@ -401,7 +401,7 @@
             pltpu.VMEM((cells, ch), bf16),
             pltpu.VMEM((width, 2 * cells + 128), bf16),
             pltpu.VMEM((width, width + 2 * cells), bf16),
-            pltpu.VMEM((width, 128), f32),
+            pltpu.VMEM((width, width), bf16),
             pltpu.VMEM((cells + 16, 2 * width), f32),
             pltpu.VMEM((width, 128), f32),
         ]
@@ -412,7 +412,6 @@
         compiler_params=pltpu.CompilerParams(vmem_limit_bytes=MAIN_MB << 20),
         name="queries",
     )(
-        base,
         queries,
         center,
         *halo,
@@ -915,41 +914,45 @@
         item.wait()
 
 
-def unpack_kernel(scale, core_ref, half_ref, other_ref, small_ref, conv_ref, map_ref, hid_ref, bias_ref, in_ref, out_ref):
+def unpack_kernel(
+    scale, half_ref, other_ref, small_ref, conv_ref, map_ref, hid_ref, bias_ref, in_ref, out_ref
+):
     f32 = jnp.float32
-    blocks, rows, lanes = half_ref.shape
+    lanes = half_ref.shape[2]
     width = in_ref.shape[1]
-
-    def write(ref, lane0):
-        def conv_out(b, carry):
-            lane = pl.ds(pl.multiple_of(lane0, lanes), lanes)
-            conv_ref[b, :, lane] = ref[b].astype(f32) * scale
-            return carry
-
-        lax.fori_loop(0, 9, conv_out, 0)
-        for k in range(4):
-            lane = pl.ds(pl.multiple_of(k * rows + lane0, lanes), lanes)
-            map_ref[:, lane] = ref[9 + k].astype(f32) * scale
-            lane = pl.ds(pl.multiple_of(k % 2 * rows + lane0, lanes), lanes)
-            hid_ref[k // 2 * rows : (k // 2 + 1) * rows, lane] = ref[13 + k].astype(f32) * scale
-
-    core = core_ref[0]
-    write(half_ref, core * lanes)
-    write(other_ref, (1 - core) * lanes)
-    bias_ref[...] = small_ref[0:1, :]
-    in_ref[0:1, :] = small_ref[1:2, 0:width]
-    in_ref[1:2, :] = small_ref[1:2, width:]
-    in_ref[2:3, :] = small_ref[2:3, 0:width]
-    out_ref[...] = small_ref[2:3, width:]
+    i = pl.program_id(0)
+    core = lax.rem(lax.axis_index("lat"), 2)
+    keep = pl.ds(pl.multiple_of(core * lanes, lanes), lanes)
+    give = pl.ds(pl.multiple_of((1 - core) * lanes, lanes), lanes)
+    conv_ref[0, :, keep] = half_ref[i].astype(f32) * scale
+    conv_ref[0, :, give] = other_ref[i].astype(f32) * scale
+
+    @pl.when(i < 4)
+    def _():
+        map_ref[:, keep] = half_ref[9 + i].astype(f32) * scale
+        map_ref[:, give] = other_ref[9 + i].astype(f32) * scale
+        hid_ref[:, keep] = half_ref[13 + i].astype(f32) * scale
+        hid_ref[:, give] = other_ref[13 + i].astype(f32) * scale
+
+    @pl.when(i == 0)
+    def _():
+        bias_ref[...] = small_ref[0:1, :]
+        in_ref[0:1, :] = small_ref[1:2, 0:width]
+        in_ref[1:2, :] = small_ref[1:2, width:]
+        in_ref[2:3, :] = small_ref[2:3, 0:width]
+        out_ref[...] = small_ref[2:3, width:]
 
 
 def run_unpack(half, other, small, scale, width):
     f32 = jnp.float32
     _, ch, _ = half.shape
-    core = lax.rem(lax.axis_index("lat"), 2).astype(jnp.int32).reshape(1)
-    vmem = pl.BlockSpec(memory_space=pltpu.VMEM)
+
+    def whole(shape):
+        return pl.BlockSpec(shape, lambda i: (0,) * len(shape))
+
     return pl.pallas_call(
         functools.partial(unpack_kernel, scale),
+        grid=(9,),
         out_shape=(
             jax.ShapeDtypeStruct((9, ch, ch), f32),
             jax.ShapeDtypeStruct((ch, 2 * width), f32),
@@ -958,11 +961,18 @@
             jax.ShapeDtypeStruct((3, width), f32),
             jax.ShapeDtypeStruct((1, width), f32),
         ),
-        in_specs=[pl.BlockSpec(memory_space=pltpu.SMEM)] + [vmem] * 3,
-        out_specs=(vmem,) * 6,
+        in_specs=[whole(half.shape), whole(other.shape), whole(small.shape)],
+        out_specs=(
+            pl.BlockSpec((1, ch, ch), lambda i: (i, 0, 0)),
+            pl.BlockSpec((ch, ch), lambda i: (0, jnp.minimum(i, 3))),
+            pl.BlockSpec((ch, ch), lambda i: (jnp.minimum(i, 3) // 2, jnp.minimum(i, 3) % 2)),
+            whole((1, 2 * width)),
+            whole((3, width)),
+            whole((1, width)),
+        ),
         compiler_params=pltpu.CompilerParams(vmem_limit_bytes=24 << 20),
         name="unpack",
-    )(core, half, other, small)
+    )(half, other, small)
 
 
 def run_finish(fg, conv_weight, grads, small, tile_shape, scale, width):
@@ -1063,11 +1073,8 @@
         ]
     ).reshape(8, dev_count * group)
 
-    base = jnp.stack(
-        [lax.axis_index("lat") * rows, lax.axis_index("lon") * cols]
-    ).astype(f32)
     weights = (conv_weight, map_weight, map_bias, input_weight, hidden_weight, output_weight)
-    fg, grads, small = run_main(base, queries, latents, halo, weights, dims)
+    fg, grads, small = run_main(queries, latents, halo, weights, dims)
     scale = float(hits * group * dev_count) ** (-0.5)
     width = input_weight.shape[1]
     latent_grad, half, other, small = run_finish(

time: 109 us -> 109 us (level)
    pallas_call x1, Pallas kernels: 2.61 us -> 4.42 us  [run_unpack(): pl.pallas_call(functools.partial(unpack_kernel, scale), grid=(9,), out_sh...]
    pallas_call x1, Pallas kernels: 45.7 us -> 44 us  [run_main(): pl.pallas_call(functools.partial(main_kernel, dims), out_shape=(jax.Shape...]
where the time goes in v5:
time: 109 us
  Pallas kernels  101 us (93%)
  local copies, waits for them, and re-layouts  5.06 us (5%)
  other arithmetic  1.55 us (1%)
    pallas_call x1, Pallas kernels, run_main(): pl.pallas_call(functools.partial(main_kernel, dims), out_shape=(jax.Shape...  44 us
    pallas_call x1, Pallas kernels, run_finish(): pl.pallas_call(functools.partial(finish_kernel, (nx, ny, nz), CHUNKS, sca...  35 us
    pallas_call x1, Pallas kernels, run_front(): pl.pallas_call(front_kernel, out_shape=(jax.ShapeDtypeStruct((lat_n, lon_...  18 us
    pallas_call x1, Pallas kernels, run_unpack(): pl.pallas_call(functools.partial(unpack_kernel, scale), grid=(9,), out_sh...  4.42 us
    unnamed x19, local copies, waits for them, and re-layouts  2.29 us

profile of v5, /device:TPU:1, one launch (start us, length us, event | category | flops | bytes accessed | tf_op | source)
XLA Modules:
  0.0 108.8 jit_solution(6035705034928195804)
XLA Ops:
  0.6 0.7 multiply_bitcast_fusion
  1.3 0.8 reshape.122.cot_ref
  2.1 1.0 reshape.121.grid_ref
  3.1 0.9 copy-done.1
  4.0 0.7 copy-done.8
  4.7 0.0 copy-start.5
  4.7 0.0 copy-start.6
  4.7 0.0 copy-start.7
  4.7 18.0 %front.1 = (f32[8,16,256]{2,1,0:T(8,128)S(1)}, bf16[16,256]{1,0:T(8,128)(2,1)S(1)}, bf16[16,256]{1,0:T(8,128)(2,1)S(1)}, bf16[18,256]{1,0:T(8,128)(2,1)S(1)}, bf16[18,256]{1,0:T(8,128)(2,1)S(1)}) custom-call(s32[3,96,64]{2,1,0:T(8,128)S(1)} %reshape.121.grid_ref, f32[96,64]{1,0:T(8,128)S(1)} %reshape.122.cot_ref, s32[1,96]{1,0:T(1,128)S(1)} %bitcast.16, ...), custom_call_target="tpu_custom_call" | custom-call | tf_op jit(solution)/shard_map/front/pallas_call | solution.py:594
  22.7 0.2 reshape.125
  22.9 0.8 slice_reduce_fusion
  23.7 0.1 stack.14
  23.8 0.1 stack.13
  23.9 0.1 squeeze.14
  24.0 0.1 add.40
  24.2 0.1 multiply_subtract_fusion
  24.3 0.3 stack.16.q_ref
  24.6 0.0 copy-done
  24.6 0.0 copy-done.2
  24.6 0.0 copy-done.3
  24.7 44.0 %queries.1 = (bf16[256,256]{1,0:T(8,128)(2,1)S(1)}, f32[17,256,256]{2,1,0:T(8,128)S(1)}, f32[8,1024]{1,0:T(8,128)S(1)}) custom-call(f32[8,8192]{1,0:T(8,128)S(1)} %stack.16.q_ref, bf16[16,16,256]{2,1,0:T(8,128)(2,1)S(1)} %copy-done.2, bf16[16,256]{1,0:T(8,128)(2,1)S(1)} %get-tuple-element.26.top_ref, bf16[16,256]{1,0:T(8,128)(2,1)S(1)} %get-tuple-element.27.bottom_ref, ...), custom_call_target="tpu_custom_call" | custom-call | tf_op jit(solution)/shard_map/queries/pallas_call | solution.py:389
  68.7 35.0 %finish.1 = (f32[16,16,256]{2,1,0:T(8,128)S(1)}, bf16[17,256,128]{2,1,0:T(8,128)(2,1)S(1)}, bf16[17,256,128]{2,1,0:T(8,128)(2,1)S(1)}, f32[8,1024]{1,0:T(8,128)S(1)}) custom-call(bf16[256,256]{1,0:T(8,128)(2,1)S(1)} %get-tuple-element.30.fg_ref, bf16[9,256,256]{2,1,0:T(8,128)(2,1)S(1)} %copy-done, f32[17,256,256]{2,1,0:T(8,128)S(1)} %get-tuple-element.31.wg_ref, ...), custom_call_target="tpu_custom_call" | custom-call | tf_op jit(solution)/shard_map/finish/pallas_call | solution.py:987
  103.7 4.4 %unpack.1 = (f32[9,256,256]{2,1,0:T(8,128)}, f32[256,1024]{1,0:T(8,128)}, f32[512,512]{1,0:T(8,128)}, f32[1,1024]{1,0:T(1,128)}, f32[3,512]{1,0:T(4,128)}, /*index=5*/f32[1,512]{1,0:T(1,128)}) custom-call(bf16[17,256,128]{2,1,0:T(8,128)(2,1)S(1)} %get-tuple-element.34.half_ref, bf16[17,256,128]{2,1,0:T(8,128)(2,1)S(1)} %get-tuple-element.35.other_ref, ...), custom_call_target="tpu_custom_call" | custom-call | tf_op jit(solution)/shard_map/unpack/pallas_call | solution.py:953
  108.1 0.7 copy.23
  (12 shorter events, 0.1 us)
Async XLA Ops:
  3.1 0.9 copy-start.1
  4.0 0.7 copy-start.8
  4.7 19.9 %copy-start = (bf16[9,256,256]{2,1,0:T(8,128)(2,1)S(1)}, bf16[9,256,256]{2,1,0:T(8,128)(2,1)}, u32[]{:S(2)}) copy-start(bf16[9,256,256]{2,1,0:T(8,128)(2,1)} %convw_ref.1) | copy-start | bytes 3538948
  4.7 19.9 %copy-start.2 = (bf16[16,16,256]{2,1,0:T(8,128)(2,1)S(1)}, bf16[16,16,256]{2,1,0:T(8,128)(2,1)}, u32[]{:S(2)}) copy-start(bf16[16,16,256]{2,1,0:T(8,128)(2,1)} %center_ref.1) | copy-start | bytes 393220
  4.7 19.9 %copy-start.3 = (bf16[256,1024]{1,0:T(8,128)(2,1)S(1)}, bf16[256,1024]{1,0:T(8,128)(2,1)}, u32[]{:S(2)}) copy-start(bf16[256,1024]{1,0:T(8,128)(2,1)} %mapw_ref.1) | copy-start | bytes 1572868
  4.7 20.0 %copy-start.4 = (bf16[1,512,512]{2,1,0:T(8,128)(2,1)S(1)}, bf16[1,512,512]{2,1,0:T(8,128)(2,1)}, u32[]{:S(2)}) copy-start(bf16[1,512,512]{2,1,0:T(8,128)(2,1)} %param.16) | copy-start | bytes 1572868
  4.7 20.0 %copy-start.5 = (f32[3,512]{1,0:T(4,128)S(1)}, f32[3,512]{1,0:T(4,128)}, u32[]{:S(2)}) copy-start(f32[3,512]{1,0:T(4,128)} %inw_ref.1) | copy-start | bytes 18436
  4.7 20.0 %copy-start.6 = (f32[1024]{0:T(1024)S(1)}, f32[1024]{0:T(1024)}, u32[]{:S(2)}) copy-start(f32[1024]{0:T(1024)} %param.14) | copy-start | bytes 12292
  4.7 20.0 %copy-start.7 = (f32[512]{0:T(512)S(1)}, f32[512]{0:T(512)}, u32[]{:S(2)}) copy-start(f32[512]{0:T(512)} %param.17) | copy-start | bytes 6148

commit v6 on v4

--- a/solution.py
+++ b/solution.py
@@ -96,7 +96,6 @@
 
 def main_kernel(
     dims,
-    base_ref,
     q_ref,
     center_ref,
     top_ref,
@@ -117,7 +116,7 @@
     feat_ref,
     tab0_ref,
     tab1_ref,
-    wcol_ref,
+    hidw_ref,
     g_ref,
     og_ref,
     *pairs,
@@ -145,8 +144,10 @@
     cell = lax.broadcasted_iota(jnp.int32, (cells, width), 0)
     row_f = (cell // cols).astype(f32)
     col_f = (cell % cols).astype(f32)
-    lat_c = ((base_ref[0] + row_f) * SUB + 0.5) * (2.0 / (lat_cells * SUB)) - 1.0
-    lon_c = ((base_ref[1] + col_f) * SUB + 0.5) * (2.0 / (lon_cells * SUB)) - 1.0
+    lat0 = (lax.axis_index("lat") * rows).astype(f32)
+    lon0 = (lax.axis_index("lon") * cols).astype(f32)
+    lat_c = ((lat0 + row_f) * SUB + 0.5) * (2.0 / (lat_cells * SUB)) - 1.0
+    lon_c = ((lon0 + col_f) * SUB + 0.5) * (2.0 / (lon_cells * SUB)) - 1.0
     lev_c = 1.0 / LEVELS - 1.0
     linear = (
         lat_c * inw_ref[0:1, :] + lon_c * inw_ref[1:2, :] + lev_c * inw_ref[2:3, :]
@@ -174,7 +175,7 @@
         for c in range(3):
             ext = jnp.where(ext_row == level * 3 + c, parts[c][level], ext)
     tab0_ref[:, 2 * cells : 2 * cells + 128] = ext.T.astype(bf16)
-    wcol_ref[...] = jnp.broadcast_to(outw_ref[...], (128, width)).T
+    hidw_ref[...] = (hid_ref[...].astype(f32) * outw_ref[...]).astype(bf16)
 
     oh0 = width
     oh1 = width + cells
@@ -226,7 +227,7 @@
     def back_dot(k):
         k = k % 4
 
-        return dots(te_ref, hid_ref, d_refs[k], slice(width, 2 * width))
+        return dots(te_ref, hidw_ref, d_refs[k], slice(width, 2 * width))
 
     def first_sine(k):
         k = k % 4
@@ -250,13 +251,10 @@
                 s, c = sincos_turns(tc_ref[m : m + ROWS, :] * INV_TURN)
                 sw = s * cot
                 cc = c * cot
-                w = wcol_ref[m : m + ROWS, :]
                 og = og_ref[m : m + ROWS, :]
                 for n in range(0, tile, 128):
                     og = og + sw[:, n : n + 128]
-                    d_refs[k][width + m : width + m + ROWS, n : n + 128] = (
-                        cc[:, n : n + 128] * w
-                    ).astype(bf16)
+                d_refs[k][width + m : width + m + ROWS, :] = cc.astype(bf16)
                 og_ref[m : m + ROWS, :] = og
 
             return run
@@ -346,6 +344,8 @@
     for u in range(4):
         stage(u, tiles - 4 + u, 4 - u)
 
+    hidg_ref[...] = hidg_ref[...] * outw_ref[...]
+    g_ref[:, width:] = g_ref[:, width:] * outw_ref[...]
     g = g_ref[0:cells, :]
     hi, lo = split2(g)
     fg = (dot_nt(hi, mapw_ref[...]) + dot_nt(lo, mapw_ref[...])).astype(bf16)
@@ -378,7 +378,7 @@
     small_ref[2:3, width:] = og
 
 
-def run_main(base, queries, center, halo, weights, dims):
+def run_main(queries, center, halo, weights, dims):
     conv_weight, map_weight, map_bias, input_weight, hidden_weight, output_weight = weights
     rows, cols, ch = center.shape
     cells = rows * cols
@@ -393,7 +393,7 @@
             jax.ShapeDtypeStruct((17, ch, ch), f32),
             jax.ShapeDtypeStruct((8, 2 * width), f32),
         ),
-        in_specs=[pl.BlockSpec(memory_space=pltpu.SMEM)] + [vmem] * 12,
+        in_specs=[vmem] * 12,
         out_specs=(vmem,) * 3,
         scratch_shapes=[
             pltpu.VMEM((width, width), f32),
@@ -401,7 +401,7 @@
             pltpu.VMEM((cells, ch), bf16),
             pltpu.VMEM((width, 2 * cells + 128), bf16),
             pltpu.VMEM((width, width + 2 * cells), bf16),
-            pltpu.VMEM((width, 128), f32),
+            pltpu.VMEM((width, width), bf16),
             pltpu.VMEM((cells + 16, 2 * width), f32),
             pltpu.VMEM((width, 128), f32),
         ]
@@ -412,7 +412,6 @@
         compiler_params=pltpu.CompilerParams(vmem_limit_bytes=MAIN_MB << 20),
         name="queries",
     )(
-        base,
         queries,
         center,
         *halo,
@@ -915,7 +914,7 @@
         item.wait()
 
 
-def unpack_kernel(scale, core_ref, half_ref, other_ref, small_ref, conv_ref, map_ref, hid_ref, bias_ref, in_ref, out_ref):
+def unpack_kernel(scale, half_ref, other_ref, small_ref, conv_ref, map_ref, hid_ref, bias_ref, in_ref, out_ref):
     f32 = jnp.float32
     blocks, rows, lanes = half_ref.shape
     width = in_ref.shape[1]
@@ -933,7 +932,7 @@
             lane = pl.ds(pl.multiple_of(k % 2 * rows + lane0, lanes), lanes)
             hid_ref[k // 2 * rows : (k // 2 + 1) * rows, lane] = ref[13 + k].astype(f32) * scale
 
-    core = core_ref[0]
+    core = lax.rem(lax.axis_index("lat"), 2)
     write(half_ref, core * lanes)
     write(other_ref, (1 - core) * lanes)
     bias_ref[...] = small_ref[0:1, :]
@@ -946,7 +945,6 @@
 def run_unpack(half, other, small, scale, width):
     f32 = jnp.float32
     _, ch, _ = half.shape
-    core = lax.rem(lax.axis_index("lat"), 2).astype(jnp.int32).reshape(1)
     vmem = pl.BlockSpec(memory_space=pltpu.VMEM)
     return pl.pallas_call(
         functools.partial(unpack_kernel, scale),
@@ -958,11 +956,11 @@
             jax.ShapeDtypeStruct((3, width), f32),
             jax.ShapeDtypeStruct((1, width), f32),
         ),
-        in_specs=[pl.BlockSpec(memory_space=pltpu.SMEM)] + [vmem] * 3,
+        in_specs=[vmem] * 3,
         out_specs=(vmem,) * 6,
         compiler_params=pltpu.CompilerParams(vmem_limit_bytes=24 << 20),
         name="unpack",
-    )(core, half, other, small)
+    )(half, other, small)
 
 
 def run_finish(fg, conv_weight, grads, small, tile_shape, scale, width):
@@ -1063,11 +1061,8 @@
         ]
     ).reshape(8, dev_count * group)
 
-    base = jnp.stack(
-        [lax.axis_index("lat") * rows, lax.axis_index("lon") * cols]
-    ).astype(f32)
     weights = (conv_weight, map_weight, map_bias, input_weight, hidden_weight, output_weight)
-    fg, grads, small = run_main(base, queries, latents, halo, weights, dims)
+    fg, grads, small = run_main(queries, latents, halo, weights, dims)
     scale = float(hits * group * dev_count) ** (-0.5)
     width = input_weight.shape[1]
     latent_grad, half, other, small = run_finish(

time: 109 us -> 107 us (0.982)
  Pallas kernels: 101 us -> 99.6 us
    pallas_call x1, Pallas kernels: 45.7 us -> 44 us  [run_main(): pl.pallas_call(functools.partial(main_kernel, dims), out_shape=(jax.Shape...]
where the time goes in v6:
time: 107 us
  Pallas kernels  99.6 us (93%)
  local copies, waits for them, and re-layouts  5.06 us (5%)
  other arithmetic  1.55 us (1%)
    pallas_call x1, Pallas kernels, run_main(): pl.pallas_call(functools.partial(main_kernel, dims), out_shape=(jax.Shape...  44 us
    pallas_call x1, Pallas kernels, run_finish(): pl.pallas_call(functools.partial(finish_kernel, (nx, ny, nz), CHUNKS, sca...  35 us
    pallas_call x1, Pallas kernels, run_front(): pl.pallas_call(front_kernel, out_shape=(jax.ShapeDtypeStruct((lat_n, lon_...  18 us
    pallas_call x1, Pallas kernels, run_unpack(): pl.pallas_call(functools.partial(unpack_kernel, scale), out_shape=(jax.Sh...  2.62 us
    unnamed x19, local copies, waits for them, and re-layouts  2.3 us

profile of v6, /device:TPU:1, one launch (start us, length us, event | category | flops | bytes accessed | tf_op | source)
XLA Modules:
  0.0 107.0 jit_solution(10613980784102002992)
XLA Ops:
  0.6 0.7 multiply_bitcast_fusion
  1.3 0.8 reshape.122.cot_ref
  2.1 1.0 reshape.121.grid_ref
  3.1 0.9 copy-done.1
  4.0 0.7 copy-done.8
  4.7 0.0 copy-start.5
  4.7 0.0 copy-start.6
  4.7 0.0 copy-start.7
  4.7 18.0 %front.1 = (f32[8,16,256]{2,1,0:T(8,128)S(1)}, bf16[16,256]{1,0:T(8,128)(2,1)S(1)}, bf16[16,256]{1,0:T(8,128)(2,1)S(1)}, bf16[18,256]{1,0:T(8,128)(2,1)S(1)}, bf16[18,256]{1,0:T(8,128)(2,1)S(1)}) custom-call(s32[3,96,64]{2,1,0:T(8,128)S(1)} %reshape.121.grid_ref, f32[96,64]{1,0:T(8,128)S(1)} %reshape.122.cot_ref, s32[1,96]{1,0:T(1,128)S(1)} %bitcast.16, ...), custom_call_target="tpu_custom_call" | custom-call | tf_op jit(solution)/shard_map/front/pallas_call | solution.py:594
  22.7 0.2 reshape.125
  22.9 0.8 slice_reduce_fusion
  23.7 0.1 stack.14
  23.8 0.1 stack.13
  23.9 0.1 squeeze.14
  24.0 0.1 add.40
  24.2 0.1 multiply_subtract_fusion
  24.3 0.3 stack.16.q_ref
  24.6 0.0 copy-done
  24.6 0.0 copy-done.2
  24.6 0.0 copy-done.3
  24.7 44.0 %queries.1 = (bf16[256,256]{1,0:T(8,128)(2,1)S(1)}, f32[17,256,256]{2,1,0:T(8,128)S(1)}, f32[8,1024]{1,0:T(8,128)S(1)}) custom-call(f32[8,8192]{1,0:T(8,128)S(1)} %stack.16.q_ref, bf16[16,16,256]{2,1,0:T(8,128)(2,1)S(1)} %copy-done.2, bf16[16,256]{1,0:T(8,128)(2,1)S(1)} %get-tuple-element.26.top_ref, bf16[16,256]{1,0:T(8,128)(2,1)S(1)} %get-tuple-element.27.bottom_ref, ...), custom_call_target="tpu_custom_call" | custom-call | tf_op jit(solution)/shard_map/queries/pallas_call | solution.py:389
  68.7 35.0 %finish.1 = (f32[16,16,256]{2,1,0:T(8,128)S(1)}, bf16[17,256,128]{2,1,0:T(8,128)(2,1)S(1)}, bf16[17,256,128]{2,1,0:T(8,128)(2,1)S(1)}, f32[8,1024]{1,0:T(8,128)S(1)}) custom-call(bf16[256,256]{1,0:T(8,128)(2,1)S(1)} %get-tuple-element.30.fg_ref, bf16[9,256,256]{2,1,0:T(8,128)(2,1)S(1)} %copy-done, f32[17,256,256]{2,1,0:T(8,128)S(1)} %get-tuple-element.31.wg_ref, ...), custom_call_target="tpu_custom_call" | custom-call | tf_op jit(solution)/shard_map/finish/pallas_call | solution.py:975
  103.7 2.6 %unpack.1 = (f32[9,256,256]{2,1,0:T(8,128)}, f32[256,1024]{1,0:T(8,128)}, f32[512,512]{1,0:T(8,128)}, f32[1,1024]{1,0:T(1,128)}, f32[3,512]{1,0:T(4,128)}, /*index=5*/f32[1,512]{1,0:T(1,128)}) custom-call(bf16[17,256,128]{2,1,0:T(8,128)(2,1)S(1)} %get-tuple-element.34.half_ref, bf16[17,256,128]{2,1,0:T(8,128)(2,1)S(1)} %get-tuple-element.35.other_ref, ...), custom_call_target="tpu_custom_call" | custom-call | tf_op jit(solution)/shard_map/unpack/pallas_call | solution.py:949
  106.3 0.7 copy.23
  (12 shorter events, 0.1 us)
Async XLA Ops:
  3.1 0.9 copy-start.1
  4.0 0.7 copy-start.8
  4.7 19.9 %copy-start = (bf16[9,256,256]{2,1,0:T(8,128)(2,1)S(1)}, bf16[9,256,256]{2,1,0:T(8,128)(2,1)}, u32[]{:S(2)}) copy-start(bf16[9,256,256]{2,1,0:T(8,128)(2,1)} %convw_ref.1) | copy-start | bytes 3538948
  4.7 19.9 %copy-start.2 = (bf16[16,16,256]{2,1,0:T(8,128)(2,1)S(1)}, bf16[16,16,256]{2,1,0:T(8,128)(2,1)}, u32[]{:S(2)}) copy-start(bf16[16,16,256]{2,1,0:T(8,128)(2,1)} %center_ref.1) | copy-start | bytes 393220
  4.7 19.9 %copy-start.3 = (bf16[256,1024]{1,0:T(8,128)(2,1)S(1)}, bf16[256,1024]{1,0:T(8,128)(2,1)}, u32[]{:S(2)}) copy-start(bf16[256,1024]{1,0:T(8,128)(2,1)} %mapw_ref.1) | copy-start | bytes 1572868
  4.7 20.0 %copy-start.4 = (bf16[1,512,512]{2,1,0:T(8,128)(2,1)S(1)}, bf16[1,512,512]{2,1,0:T(8,128)(2,1)}, u32[]{:S(2)}) copy-start(bf16[1,512,512]{2,1,0:T(8,128)(2,1)} %param.16) | copy-start | bytes 1572868
  4.7 20.0 %copy-start.5 = (f32[3,512]{1,0:T(4,128)S(1)}, f32[3,512]{1,0:T(4,128)}, u32[]{:S(2)}) copy-start(f32[3,512]{1,0:T(4,128)} %inw_ref.1) | copy-start | bytes 18436
  4.7 20.0 %copy-start.6 = (f32[1024]{0:T(1024)S(1)}, f32[1024]{0:T(1024)}, u32[]{:S(2)}) copy-start(f32[1024]{0:T(1024)} %param.14) | copy-start | bytes 12292
  4.7 20.0 %copy-start.7 = (f32[512]{0:T(512)S(1)}, f32[512]{0:T(512)}, u32[]{:S(2)}) copy-start(f32[512]{0:T(512)} %param.17) | copy-start | bytes 6148
